TPU v7x, 32 devices: a whole 2x2x4 slice. The times are simulated.
32 devices in a mesh: ra: 4 (over x, core), rb: 8 (over z, y).
Axes of the slice: x: 2, y: 2, z: 4, core: 2. Of those that a mesh axis runs over, the one named last changes fastest.
Arguments:
- features_a: bfloat16 [8, 128, 1024], P('ra', 'rb'), may hold values from -600 to 600
- features_b: bfloat16 [16, 128, 1024], P('rb', 'ra'), may hold values from -600 to 600
- weight_one: bfloat16 [16, 81], replicated, may hold values from -16 to 16
- bias_one: float32 [16], replicated, may hold values from -3 to 3
- weight_two: bfloat16 [16, 81], replicated, may hold values from -0.25 to 0.25
- bias_two: float32 [1], replicated, may hold values from -3 to 3
Outputs:
- consensus: float32 [8, 128, 16, 128], P('ra', None, 'rb')
All inputs are finite; a program needn't handle non-finite values.
Results may differ from a plain program's by a relative error of at most 0.0053.
Values may be sent and summed in bfloat16 or wider, within the bound.
No kernel may reach another device: no remote copies, remote signals or barrier semaphores. Data moves between devices by JAX's collectives and lax.ppermute only.
A program may use at most 192 MiB of HBM per device.

v0:
```python
import functools

import jax
import jax.numpy as jnp
import numpy as np
from jax import lax
from jax.experimental import pallas as pl
from jax.experimental.pallas import tpu as pltpu
from jax.sharding import PartitionSpec as P


WIN = 16
STEP = WIN - 2
VMEM = pltpu.VMEM
SMEM = pltpu.SMEM


def swap(block, axis, mask):
    count = lax.axis_size(axis)
    return lax.ppermute(block, axis, [(i, i ^ mask) for i in range(count)])


def neighbours(block, axis):
    count = lax.axis_size(axis)
    across = [(i, i + 1) for i in range(1, count - 1, 2)]
    far = lax.ppermute(block, axis, across + [(j, i) for i, j in across])
    return swap(block, axis, 1), far


def gathered(block, axis):
    count = lax.axis_size(axis)
    even = jnp.stack([block] + [swap(block, axis, mask) for mask in range(2, count, 2)])
    return even, swap(even, axis, 1)


def normalize(values):
    values = values.astype(jnp.float32)
    scale = lax.rsqrt(jnp.sum(values * values, axis=-1, keepdims=True) + 1e-06)
    return (values * scale).astype(jnp.bfloat16)


def corr_kernel(a_even, a_odd, b_even, b_odd, out, all_a, all_b):
    at_a, at_b = lax.axis_index("ra"), lax.axis_index("rb")
    odd = at_b & 1
    rows_b = b_even.shape[2]
    ext = all_b.shape[0]
    near_from = (1 - odd) * (ext - 2)
    far_from = odd * (ext - 2)
    for low, ref in enumerate((a_even, a_odd)):
        cols = ref.shape[2]
        for m in range(ref.shape[0]):
            source = at_b ^ (2 * m + low)
            start = pl.multiple_of(source * cols, cols)
            all_a[:, pl.ds(start, cols), :] = normalize(ref[m]).astype(all_a.dtype)
    for low, ref in enumerate((b_even, b_odd)):
        cols = ref.shape[3]
        for m in range(ref.shape[0]):
            source = at_a ^ (2 * m + low)
            start = pl.multiple_of(source * cols, cols)
            for k in range(rows_b):
                all_b[2 + k, pl.ds(start, cols), :] = normalize(ref[m, 0, k]).astype(all_b.dtype)
            for side, begin, skip in ((1, near_from, odd), (2, far_from, 1 - odd)):
                for k in range(2):
                    row = ref[m, side, skip * (rows_b - 2) + k]
                    all_b[begin + k, pl.ds(start, cols), :] = normalize(row).astype(all_b.dtype)
    for k in range(ext):
        row_b = all_b[k].astype(jnp.bfloat16)
        for i in range(out.shape[1]):
            out[k, i] = lax.dot_general(
                all_a[i].astype(jnp.bfloat16),
                row_b,
                (((1,), (1,)), ((), ())),
                preferred_element_type=jnp.float32,
            ).astype(jnp.bfloat16)


def correlate(a_even, a_odd, b_even, b_odd):
    half_a, rows_a, cols_a, channels = a_even.shape
    half_b, _, rows_b, cols_b, _ = b_even.shape
    wide_a, wide_b = 2 * half_a * cols_a, 2 * half_b * cols_b
    kind_a = jnp.bfloat16 if cols_a % 16 == 0 else jnp.float32
    kind_b = jnp.bfloat16 if cols_b % 16 == 0 else jnp.float32
    return pl.pallas_call(
        corr_kernel,
        out_shape=jax.ShapeDtypeStruct((rows_b + 4, rows_a, wide_a, wide_b), jnp.bfloat16),
        in_specs=[pl.BlockSpec(memory_space=VMEM)] * 4,
        out_specs=pl.BlockSpec(memory_space=VMEM),
        scratch_shapes=[
            VMEM((rows_a, wide_a, channels), kind_a),
            VMEM((rows_b + 4, wide_b, channels), kind_b),
        ],
        name="correlate",
    )(a_even, a_odd, b_even, b_odd)


def band_tables(hid):
    taps = np.arange(81)
    ta, tb, tc, td = taps // 27, taps // 9 % 3, taps // 3 % 3, taps % 3
    col = np.arange(27 * WIN)
    ca, cc, cd, cw = col // (9 * WIN), col // (3 * WIN) % 3, col // WIN % 3, col % WIN
    pick = np.zeros((3, 81, 27 * WIN), np.float32)
    for b in range(3):
        pick[b] = (
            (tb[:, None] == b)
            & (ta[:, None] == ca[None])
            & (tc[:, None] == cc[None])
            & (td[:, None] == cd[None])
        )
    row = np.arange(hid * STEP)
    ro, rj = row // STEP, row % STEP
    grow = (ro[:, None] == np.arange(hid)[None]).astype(np.float32)
    return pick, grow, cw, rj


def band_kernel(pick, grow, w1, w2, bias, tail, band1, band2, bias_full):
    rows, cols = band1.shape
    jj = lax.broadcasted_iota(jnp.int32, (rows, cols), 0) % STEP
    ww = lax.broadcasted_iota(jnp.int32, (rows, cols), 1) % WIN
    total = jnp.zeros((rows, cols), jnp.float32)
    for b in range(3):
        wide = jnp.dot(w1[...], pick[b], preferred_element_type=jnp.float32).astype(jnp.bfloat16)
        tall = jnp.dot(grow[...], wide, preferred_element_type=jnp.float32)
        total = total + jnp.where(ww - jj == b, tall, 0.0)
    band1[...] = total.astype(jnp.bfloat16)
    jj = lax.broadcasted_iota(jnp.int32, (cols, rows), 1) % STEP
    rr = lax.broadcasted_iota(jnp.int32, (cols, rows), 0) % WIN
    total = jnp.zeros((cols, rows), jnp.float32)
    for b in range(3):
        wide = lax.dot_general(
            pick[b], w2[...], (((0,), (1,)), ((), ())), preferred_element_type=jnp.float32
        ).astype(jnp.bfloat16)
        tall = lax.dot_general(
            wide, grow[...], (((1,), (1,)), ((), ())), preferred_element_type=jnp.float32
        )
        total = total + jnp.where(jj - rr + 2 == b, tall, 0.0)
    band2[0] = total.astype(jnp.bfloat16)
    band2[1] = jnp.where(jj < tail, total, 0.0).astype(jnp.bfloat16)
    bias_full[...] = jnp.broadcast_to(
        lax.dot_general(
            grow[...].astype(jnp.float32),
            bias[...],
            (((1,), (0,)), ((), ())),
            precision=lax.Precision.HIGHEST,
            preferred_element_type=jnp.float32,
        ),
        bias_full.shape,
    )


def bands(weight_one, bias_one, weight_two, width):
    hid = weight_one.shape[0]
    pick, grow, _, _ = band_tables(hid)
    blocks = pl.cdiv(width, STEP)
    tail = width - STEP * (blocks - 1)

    def body(pick, grow, w1, w2, bias, band1, band2, bias_full):
        band_kernel(pick, grow, w1, w2, bias, tail, band1, band2, bias_full)

    return pl.pallas_call(
        body,
        out_shape=(
            jax.ShapeDtypeStruct((hid * STEP, 27 * WIN), jnp.bfloat16),
            jax.ShapeDtypeStruct((2, 27 * WIN, hid * STEP), jnp.bfloat16),
            jax.ShapeDtypeStruct((hid * STEP, 128), jnp.float32),
        ),
        in_specs=[pl.BlockSpec(memory_space=VMEM)] * 5,
        out_specs=(pl.BlockSpec(memory_space=VMEM),) * 3,
        name="bands",
    )(
        jnp.asarray(pick, jnp.bfloat16),
        jnp.asarray(grow, jnp.bfloat16),
        weight_one,
        weight_two,
        jnp.broadcast_to(bias_one[:, None], (hid, 128)),
    )


def shifted(values, by):
    lane = lax.broadcasted_iota(jnp.int32, values.shape, values.ndim - 1)
    width = values.shape[-1]
    if by == 1:
        return jnp.where(lane == 0, 0.0, pltpu.roll(values, 1, values.ndim - 1))
    return jnp.where(lane == width - 1, 0.0, pltpu.roll(values, width - 1, values.ndim - 1))


def conv_kernel(n_a, n_b, own, near, far, band1, band2, bias1, bias2, out, stage, window_a, window_b, total):
    ext_k, rows_a, width, lanes = own.shape
    rows_b = ext_k - 4
    hid_i, hid_k = rows_a + 2, rows_b + 2
    pairs = hid_k // 2
    blocks = pl.cdiv(width, STEP)
    at_a, at_b = lax.axis_index("ra"), lax.axis_index("rb")
    odd = at_a & 1

    def inside(at, count, rows, row):
        where = at * rows + row - 1
        return ((where >= 0) & (where < count * rows)).astype(jnp.float32)

    valid_i = [inside(at_a, n_a, rows_a, i) for i in range(hid_i)]
    valid_k = [inside(at_b, n_b, rows_b, k) for k in range(hid_k)]
    total[...] = jnp.zeros_like(total)

    def fill(k, carry):
        for i in range(rows_a + 4):
            stage[i, k, 0:8, :] = jnp.zeros((8, lanes), jnp.float32)
            stage[i, k, 8 + width :, :] = jnp.zeros((stage.shape[2] - 8 - width, lanes), jnp.float32)
        for i in range(rows_a):
            stage[2 + i, k, 8 : 8 + width, :] = own[k, i].astype(jnp.float32)
        for i in range(2):
            row = near[k, odd * (rows_a - 2) + i]
            stage[(1 - odd) * (rows_a + 2) + i, k, 8 : 8 + width, :] = row.astype(jnp.float32)
            row = far[k, (1 - odd) * (rows_a - 2) + i]
            stage[odd * (rows_a + 2) + i, k, 8 : 8 + width, :] = row.astype(jnp.float32)
        return carry

    lax.fori_loop(0, ext_k, fill, 0)

    def build(block, window, rows):
        for i in rows:
            for k in range(ext_k):
                tall = stage[i, k, pl.ds(STEP * block + 7, WIN), :]
                for d, piece in enumerate((shifted(tall, 1), tall, shifted(tall, -1))):
                    window[i, k, d] = piece.astype(jnp.bfloat16)

    def convolve_block(block, window, following):
        last = (block == blocks - 1).astype(jnp.int32)
        sums = {}

        def first(i):
            columns = jnp.concatenate(
                [
                    jnp.concatenate(
                        [window[i + a, k : k + 3].reshape(9 * WIN, lanes) for a in range(3)], axis=0
                    )
                    for k in range(hid_k)
                ],
                axis=1,
            )
            hidden = jnp.dot(band1[...], columns, preferred_element_type=jnp.float32)
            bias = bias1[...]
            return jnp.maximum(hidden + jnp.concatenate([bias] * hid_k, axis=1), 0.0).astype(jnp.bfloat16)

        def second(i, hidden):
            taps_a = [a for a in range(3) if 1 <= i - a + 1 <= rows_a]
            for p in range(pairs):
                k = 2 * p
                taps_c = [c for c in range(3) if any(1 <= k + h - c + 1 <= rows_b for h in range(2))]
                size = 3 * WIN
                weights = jnp.concatenate(
                    [band2[last, pl.ds((3 * a + c) * size, size), :] for a in taps_a for c in taps_c], axis=0
                )
                result = jnp.dot(
                    weights, hidden[:, k * lanes : (k + 2) * lanes], preferred_element_type=jnp.float32
                )
                at = 0
                for a in taps_a:
                    for c in taps_c:
                        for d in range(3):
                            for h in range(2):
                                o_i, o_k = i - a, k + h - c
                                if 0 <= o_k < rows_b:
                                    piece = result[at : at + WIN, h * lanes : (h + 1) * lanes]
                                    if i in (0, hid_i - 1) or k + h in (0, hid_k - 1):
                                        piece = piece * (valid_i[i] * valid_k[k + h])
                                    key = (o_i, o_k, d)
                                    sums[key] = sums[key] + piece if key in sums else piece
                            at += WIN

        ext_i = rows_a + 4
        held = first(0)
        following(range(0, ext_i // hid_i + 1))
        for i in range(1, hid_i):
            fresh = first(i)
            second(i - 1, held)
            following(range(ext_i * i // hid_i + 1, ext_i * (i + 1) // hid_i + 1) if i < hid_i - 1 else range(ext_i * i // hid_i + 1, ext_i))
            held = fresh
        second(hid_i - 1, held)
        for o_i in range(rows_a):
            for o_k in range(rows_b):
                rows = pl.ds(STEP * block + 7, WIN)
                total[o_i, o_k, rows, :] = total[o_i, o_k, rows, :] + (
                    shifted(sums[o_i, o_k, 0], 1) + sums[o_i, o_k, 1] + shifted(sums[o_i, o_k, 2], -1)
                )

    build(0, window_a, range(rows_a + 4))

    def two(step, carry):
        block = 2 * step
        convolve_block(block, window_a, lambda rows: build(block + 1, window_b, rows))
        convolve_block(block + 1, window_b, lambda rows: build(block + 2, window_a, rows))
        return carry

    lax.fori_loop(0, blocks // 2, two, 0)
    for o_i in range(rows_a):
        for o_k in range(rows_b):
            out[o_i, :, o_k, :] = jnp.maximum(total[o_i, o_k, 8 : 8 + width, :] + bias2[0], 0.0)


def convolve(n_a, n_b, own, near, far, band1, band2, bias_full, bias_two):
    ext_k, rows_a, width, lanes = own.shape
    rows_b = ext_k - 4
    blocks = pl.cdiv(width, STEP)
    assert blocks % 2 == 0
    tall = pl.cdiv(STEP * blocks + 7 + WIN, 8) * 8
    window = VMEM((rows_a + 4, ext_k, 3, WIN, lanes), jnp.bfloat16)
    return pl.pallas_call(
        functools.partial(conv_kernel, n_a, n_b),
        out_shape=jax.ShapeDtypeStruct((rows_a, width, rows_b, lanes), jnp.float32),
        in_specs=[pl.BlockSpec(memory_space=VMEM)] * 6 + [pl.BlockSpec(memory_space=SMEM)],
        out_specs=pl.BlockSpec(memory_space=VMEM),
        scratch_shapes=[
            VMEM((rows_a + 4, ext_k, tall, lanes), jnp.float32),
            window,
            window,
            VMEM((rows_a, rows_b, tall, lanes), jnp.float32),
        ],
        name="convolve",
    )(own, near, far, band1, band2, bias_full, bias_two)


def per_device(features_a, features_b, weight_one, bias_one, weight_two, bias_two):
    near_b, far_b = neighbours(features_b, "rb")
    a_even, a_odd = gathered(features_a, "rb")
    b_even, b_odd = gathered(jnp.stack([features_b, near_b, far_b]), "ra")
    tables = bands(weight_one, bias_one, weight_two, 2 * a_even.shape[0] * a_even.shape[2])
    own = correlate(a_even, a_odd, b_even, b_odd)
    near, far = neighbours(own, "ra")
    return convolve(lax.axis_size("ra"), lax.axis_size("rb"), own, near, far, *tables, bias_two)


def solution(mesh):
    return jax.shard_map(
        per_device,
        mesh=mesh,
        in_specs=(P("ra", "rb", None), P("rb", "ra", None), P(), P(), P(), P()),
        out_specs=P("ra", None, "rb", None),
        check_vma=False,
    )
```

profile of v0, /device:TPU:1, one launch (start us, length us, event | category | flops | bytes accessed | tf_op | source)
XLA Modules:
  0.0 66.1 jit_solution(16762229474234324601)
XLA Ops:
  0.0 2.1 %collective-permute-start.4 = (bf16[2,32,1024]{2,1,0:T(8,128)(2,1)}, bf16[2,32,1024]{2,1,0:T(8,128)(2,1)S(1)}, u32[]{:S(2)}, u32[]{:S(2)}) collective-permute-start(bf16[2,32,1024]{2,1,0:T(8,128)(2,1)} %param.9), channel_id=1, source_target_pairs={{0,1},{1,0},{2,3},{3,2},{4,5},{5,4},{6,7},{7,6},{8,9},{9,8},{10,11... | collective-permute-start | bytes 393224 | tf_op jit(solution)/shard_map/ppermute | solution.py:20
  2.1 0.7 collective-permute-start.5
  2.7 2.7 %collective-permute-done.4 = bf16[2,32,1024]{2,1,0:T(8,128)(2,1)S(1)} collective-permute-done((bf16[2,32,1024]{2,1,0:T(8,128)(2,1)}, bf16[2,32,1024]{2,1,0:T(8,128)(2,1)S(1)}, u32[]{:S(2)}, u32[]{:S(2)}) %collective-permute-start.4) | collective-permute-done | bytes 131104 | tf_op jit(solution)/shard_map/ppermute | solution.py:20
  5.5 1.0 %fusion = (bf16[1,3,2,32,1024]{4,3,2,1,0:T(8,128)(2,1)S(1)}, bf16[3,2,32,1024]{3,2,1,0:T(8,128)(2,1)S(1)}) fusion(bf16[1,2,32,1024]{3,2,1,0:T(8,128)(2,1)S(1)} %bitcast.13, bf16[1,2,32,1024]{3,2,1,0:T(8,128)(2,1)S(1)} %bitcast.12, bf16[1,2,32,1024]{3,2,1,0:T(8,128)(2,1)} %bitcast.11), kind=kLoop, calls=%fused_computation.3 | loop fusion | flops 393216 | bytes 1179648 | tf_op jit(solution)/shard_map/stack | solution.py:32
  6.4 1.2 %collective-permute-start.6 = (bf16[3,2,32,1024]{3,2,1,0:T(8,128)(2,1)S(1)}, bf16[3,2,32,1024]{3,2,1,0:T(8,128)(2,1)S(1)}, u32[]{:S(2)}, u32[]{:S(2)}) collective-permute-start(bf16[3,2,32,1024]{3,2,1,0:T(8,128)(2,1)S(1)} %get-tuple-element.12), channel_id=1, source_target_pairs={{0,16},{8,24},{16,0},{24,8},{1,17},{9,25},{17,1},{25,9},{2,18},{10... | collective-permute-start | bytes 1179656 | tf_op jit(solution)/shard_map/ppermute | solution.py:20
  7.7 8.3 %collective-permute-done.6 = bf16[3,2,32,1024]{3,2,1,0:T(8,128)(2,1)S(1)} collective-permute-done((bf16[3,2,32,1024]{3,2,1,0:T(8,128)(2,1)S(1)}, bf16[3,2,32,1024]{3,2,1,0:T(8,128)(2,1)S(1)}, u32[]{:S(2)}, u32[]{:S(2)}) %collective-permute-start.6) | collective-permute-done | bytes 393248 | tf_op jit(solution)/shard_map/ppermute | solution.py:20
  15.9 0.1 pad_maximum_fusion.b_even
  16.0 2.2 %collective-permute-start.7 = (bf16[2,3,2,32,1024]{4,3,2,1,0:T(8,128)(2,1)S(1)}, bf16[2,3,2,32,1024]{4,3,2,1,0:T(8,128)(2,1)S(1)}, u32[]{:S(2)}, u32[]{:S(2)}) collective-permute-start(bf16[2,3,2,32,1024]{4,3,2,1,0:T(8,128)(2,1)S(1)} %pad_maximum_fusion.b_even), channel_id=1, source_target_pairs={{0,8},{8,0},{16,24},{24,16},{1,9},{9,1},{17,25},{25,17},{2,10},{10... | collective-permute-start | bytes 2359304 | tf_op jit(solution)/shard_map/ppermute | solution.py:20
  18.2 4.7 %collective-permute-start = (bf16[2,16,1024]{2,1,0:T(8,128)(2,1)S(1)}, bf16[2,16,1024]{2,1,0:T(8,128)(2,1)S(1)}, u32[]{:S(2)}, u32[]{:S(2)}) collective-permute-start(bf16[2,16,1024]{2,1,0:T(8,128)(2,1)S(1)} %copy-done.6), channel_id=1, source_target_pairs={{0,2},{1,3},{2,0},{3,1},{4,6},{5,7},{6,4},{7,5},{8,10},{9,11},{10,... | collective-permute-start | bytes 196616 | tf_op jit(solution)/shard_map/ppermute | solution.py:20
  22.9 2.3 %collective-permute-start.1 = (bf16[2,16,1024]{2,1,0:T(8,128)(2,1)S(1)}, bf16[2,16,1024]{2,1,0:T(8,128)(2,1)S(1)}, u32[]{:S(2)}, u32[]{:S(2)}) collective-permute-start(bf16[2,16,1024]{2,1,0:T(8,128)(2,1)S(1)} %copy-done.6), channel_id=1, source_target_pairs={{0,4},{1,5},{2,6},{3,7},{4,0},{5,1},{6,2},{7,3},{8,12},{9,13},{10,... | collective-permute-start | bytes 196616 | tf_op jit(solution)/shard_map/ppermute | solution.py:20
  25.2 2.3 %collective-permute-done.1 = bf16[2,16,1024]{2,1,0:T(8,128)(2,1)S(1)} collective-permute-done((bf16[2,16,1024]{2,1,0:T(8,128)(2,1)S(1)}, bf16[2,16,1024]{2,1,0:T(8,128)(2,1)S(1)}, u32[]{:S(2)}, u32[]{:S(2)}) %collective-permute-start.1) | collective-permute-done | bytes 65568 | tf_op jit(solution)/shard_map/ppermute | solution.py:20
  27.5 2.7 %collective-permute-done.2 = bf16[2,16,1024]{2,1,0:T(8,128)(2,1)S(1)} collective-permute-done((bf16[2,16,1024]{2,1,0:T(8,128)(2,1)S(1)}, bf16[2,16,1024]{2,1,0:T(8,128)(2,1)S(1)}, u32[]{:S(2)}, u32[]{:S(2)}) %collective-permute-start.2) | collective-permute-done | bytes 65568 | tf_op jit(solution)/shard_map/ppermute | solution.py:20
  30.3 0.1 collective-permute-start.3
  30.3 5.6 %collective-permute-done.3.a_odd = bf16[4,2,16,1024]{3,2,1,0:T(8,128)(2,1)S(1)} collective-permute-done((bf16[4,2,16,1024]{3,2,1,0:T(8,128)(2,1)S(1)}, bf16[4,2,16,1024]{3,2,1,0:T(8,128)(2,1)S(1)}, u32[]{:S(2)}, u32[]{:S(2)}) %collective-permute-start.3) | collective-permute-done | bytes 262176 | tf_op jit(solution)/shard_map/ppermute | solution.py:20
  35.9 0.7 %copy-done.5 = bf16[4,2,16,1024]{3,2,1,0:T(8,128)(2,1)} copy-done((bf16[4,2,16,1024]{3,2,1,0:T(8,128)(2,1)}, bf16[4,2,16,1024]{3,2,1,0:T(8,128)(2,1)S(1)}, u32[]{:S(2)}) %copy-start.5) | copy-done | bytes 262168
  36.6 0.9 %copy-done.2 = bf16[2,3,2,32,1024]{4,3,2,1,0:T(8,128)(2,1)} copy-done((bf16[2,3,2,32,1024]{4,3,2,1,0:T(8,128)(2,1)}, bf16[2,3,2,32,1024]{4,3,2,1,0:T(8,128)(2,1)S(1)}, u32[]{:S(2)}) %copy-start.2) | copy-done | bytes 786456
  37.5 4.0 %correlate.1.own = bf16[6,2,128,128]{3,2,1,0:T(8,128)(2,1)} custom-call(bf16[4,2,16,1024]{3,2,1,0:T(8,128)(2,1)} %copy-done.1, bf16[4,2,16,1024]{3,2,1,0:T(8,128)(2,1)} %copy-done.5, bf16[2,3,2,32,1024]{4,3,2,1,0:T(8,128)(2,1)} %copy-done, bf16[2,3,2,32,1024]{4,3,2,1,0:T(8,128)(2,1)} %copy-done.2), custom_call_target="tpu_custom_call" | custom-call | tf_op jit(solution)/shard_map/correlate/pallas_call | solution.py:83
  41.5 3.2 %collective-permute-start.8 = (bf16[6,2,128,128]{3,2,1,0:T(8,128)(2,1)}, bf16[6,2,128,128]{3,2,1,0:T(8,128)(2,1)S(1)}, u32[]{:S(2)}, u32[]{:S(2)}) collective-permute-start(bf16[6,2,128,128]{3,2,1,0:T(8,128)(2,1)} %correlate.1.own), channel_id=1, source_target_pairs={{0,8},{8,0},{16,24},{24,16},{1,9},{9,1},{17,25},{25,17},{2,10},{10... | collective-permute-start | bytes 1179656 | tf_op jit(solution)/shard_map/ppermute | solution.py:20
  44.6 3.1 %collective-permute-start.9 = (bf16[6,2,128,128]{3,2,1,0:T(8,128)(2,1)}, bf16[6,2,128,128]{3,2,1,0:T(8,128)(2,1)S(1)}, u32[]{:S(2)}, u32[]{:S(2)}) collective-permute-start(bf16[6,2,128,128]{3,2,1,0:T(8,128)(2,1)} %correlate.1.own), channel_id=1, source_target_pairs={{8,16},{16,8},{9,17},{17,9},{10,18},{18,10},{11,19},{19,11},{12,20... | collective-permute-start | bytes 1179656 | tf_op jit(solution)/shard_map/ppermute | solution.py:26
  48.4 0.7 %broadcast_in_dim.2.bias = f32[16,128]{1,0:T(8,128)} broadcast(f32[16]{0:T(128)S(1)} %copy-done.7), dimensions={0} | broadcast | bytes 8256 | tf_op jit(solution)/shard_map/broadcast_in_dim | solution.py:174
  49.1 3.0 %bands.1 = (bf16[224,432]{1,0:T(8,128)(2,1)}, bf16[2,432,224]{2,1,0:T(8,128)(2,1)}, f32[224,128]{1,0:T(8,128)}) custom-call(bf16[3,81,432]{2,1,0:T(8,128)(2,1)} %constant.4.clone.pick, bf16[224,16]{1,0:T(8,128)(2,1)} %constant.5.clone.grow, bf16[16,81]{1,0:T(8,128)(2,1)} %w1.1, bf16[16,81]{1,0:T(8,128)(2,1)} %w2.1, f32[16,128]{1,0:T(8,128)} %broadcast_in_dim.2.bias), custom_call_target="tpu_custom_call" | custom-call | tf_op jit(solution)/shard_map/bands/pallas_call | solution.py:159
  52.1 1.8 %collective-permute-done.9.far = bf16[6,2,128,128]{3,2,1,0:T(8,128)(2,1)S(1)} collective-permute-done((bf16[6,2,128,128]{3,2,1,0:T(8,128)(2,1)}, bf16[6,2,128,128]{3,2,1,0:T(8,128)(2,1)S(1)}, u32[]{:S(2)}, u32[]{:S(2)}) %collective-permute-start.9) | collective-permute-done | bytes 393248 | tf_op jit(solution)/shard_map/ppermute | solution.py:26
  53.9 0.8 %copy-done.4 = bf16[6,2,128,128]{3,2,1,0:T(8,128)(2,1)} copy-done((bf16[6,2,128,128]{3,2,1,0:T(8,128)(2,1)}, bf16[6,2,128,128]{3,2,1,0:T(8,128)(2,1)S(1)}, u32[]{:S(2)}) %copy-start.4) | copy-done | bytes 393240
  54.7 11.4 %convolve.1 = f32[2,128,2,128]{3,2,1,0:T(2,128)} custom-call(bf16[6,2,128,128]{3,2,1,0:T(8,128)(2,1)} %correlate.1.own, bf16[6,2,128,128]{3,2,1,0:T(8,128)(2,1)} %copy-done.3, bf16[6,2,128,128]{3,2,1,0:T(8,128)(2,1)} %copy-done.4, bf16[224,432]{1,0:T(8,128)(2,1)} %get-tuple-element.8.band1, bf16[2,432,224]{2,1,0:T(8,128)(2,1)} %get-tuple-element.9.band2, ...), custom_call_target="tpu_custom_call" | custom-call | tf_op jit(solution)/shard_map/convolve/pallas_call | solution.py:306
  (19 shorter events, 0.1 us)
Async XLA Ops:
  0.0 5.5 %collective-permute-start.4 = (bf16[2,32,1024]{2,1,0:T(8,128)(2,1)}, bf16[2,32,1024]{2,1,0:T(8,128)(2,1)S(1)}, u32[]{:S(2)}, u32[]{:S(2)}) collective-permute-start(bf16[2,32,1024]{2,1,0:T(8,128)(2,1)} %param.9), channel_id=1, source_target_pairs={{0,1},{1,0},{2,3},{3,2},{4,5},{5,4},{6,7},{7,6},{8,9},{9,8},{10,11... | collective-permute-start | bytes 393224 | tf_op jit(solution)/shard_map/ppermute | solution.py:20
  2.1 3.4 %collective-permute-start.5 = (bf16[2,32,1024]{2,1,0:T(8,128)(2,1)}, bf16[2,32,1024]{2,1,0:T(8,128)(2,1)S(1)}, u32[]{:S(2)}, u32[]{:S(2)}) collective-permute-start(bf16[2,32,1024]{2,1,0:T(8,128)(2,1)} %param.9), channel_id=1, source_target_pairs={{1,2},{3,4},{5,6},{2,1},{4,3},{6,5},{9,10},{11,12},{13,14},{10,9},... | collective-permute-start | bytes 393224 | tf_op jit(solution)/shard_map/ppermute | solution.py:26
  6.4 9.5 %collective-permute-start.6 = (bf16[3,2,32,1024]{3,2,1,0:T(8,128)(2,1)S(1)}, bf16[3,2,32,1024]{3,2,1,0:T(8,128)(2,1)S(1)}, u32[]{:S(2)}, u32[]{:S(2)}) collective-permute-start(bf16[3,2,32,1024]{3,2,1,0:T(8,128)(2,1)S(1)} %get-tuple-element.12), channel_id=1, source_target_pairs={{0,16},{8,24},{16,0},{24,8},{1,17},{9,25},{17,1},{25,9},{2,18},{10... | collective-permute-start | bytes 1179656 | tf_op jit(solution)/shard_map/ppermute | solution.py:20
  15.9 2.3 %copy-start.6 = (bf16[2,16,1024]{2,1,0:T(8,128)(2,1)S(1)}, bf16[2,16,1024]{2,1,0:T(8,128)(2,1)}, u32[]{:S(2)}) copy-start(bf16[2,16,1024]{2,1,0:T(8,128)(2,1)} %param.8) | copy-start | bytes 196612
  16.0 19.9 %copy-start = (bf16[2,3,2,32,1024]{4,3,2,1,0:T(8,128)(2,1)}, bf16[2,3,2,32,1024]{4,3,2,1,0:T(8,128)(2,1)S(1)}, u32[]{:S(2)}) copy-start(bf16[2,3,2,32,1024]{4,3,2,1,0:T(8,128)(2,1)S(1)} %pad_maximum_fusion.b_even) | copy-start | bytes 2359300
  16.0 19.9 %collective-permute-start.7 = (bf16[2,3,2,32,1024]{4,3,2,1,0:T(8,128)(2,1)S(1)}, bf16[2,3,2,32,1024]{4,3,2,1,0:T(8,128)(2,1)S(1)}, u32[]{:S(2)}, u32[]{:S(2)}) collective-permute-start(bf16[2,3,2,32,1024]{4,3,2,1,0:T(8,128)(2,1)S(1)} %pad_maximum_fusion.b_even), channel_id=1, source_target_pairs={{0,8},{8,0},{16,24},{24,16},{1,9},{9,1},{17,25},{25,17},{2,10},{10... | collective-permute-start | bytes 2359304 | tf_op jit(solution)/shard_map/ppermute | solution.py:20
  18.2 7.0 %collective-permute-start = (bf16[2,16,1024]{2,1,0:T(8,128)(2,1)S(1)}, bf16[2,16,1024]{2,1,0:T(8,128)(2,1)S(1)}, u32[]{:S(2)}, u32[]{:S(2)}) collective-permute-start(bf16[2,16,1024]{2,1,0:T(8,128)(2,1)S(1)} %copy-done.6), channel_id=1, source_target_pairs={{0,2},{1,3},{2,0},{3,1},{4,6},{5,7},{6,4},{7,5},{8,10},{9,11},{10,... | collective-permute-start | bytes 196616 | tf_op jit(solution)/shard_map/ppermute | solution.py:20
  22.9 4.6 %collective-permute-start.1 = (bf16[2,16,1024]{2,1,0:T(8,128)(2,1)S(1)}, bf16[2,16,1024]{2,1,0:T(8,128)(2,1)S(1)}, u32[]{:S(2)}, u32[]{:S(2)}) collective-permute-start(bf16[2,16,1024]{2,1,0:T(8,128)(2,1)S(1)} %copy-done.6), channel_id=1, source_target_pairs={{0,4},{1,5},{2,6},{3,7},{4,0},{5,1},{6,2},{7,3},{8,12},{9,13},{10,... | collective-permute-start | bytes 196616 | tf_op jit(solution)/shard_map/ppermute | solution.py:20
  25.2 5.0 %collective-permute-start.2 = (bf16[2,16,1024]{2,1,0:T(8,128)(2,1)S(1)}, bf16[2,16,1024]{2,1,0:T(8,128)(2,1)S(1)}, u32[]{:S(2)}, u32[]{:S(2)}) collective-permute-start(bf16[2,16,1024]{2,1,0:T(8,128)(2,1)S(1)} %copy-done.6), channel_id=1, source_target_pairs={{0,6},{1,7},{2,4},{3,5},{4,2},{5,3},{6,0},{7,1},{8,14},{9,15},{10,... | collective-permute-start | bytes 196616 | tf_op jit(solution)/shard_map/ppermute | solution.py:20
  30.2 5.7 %copy-start.1 = (bf16[4,2,16,1024]{3,2,1,0:T(8,128)(2,1)}, bf16[4,2,16,1024]{3,2,1,0:T(8,128)(2,1)S(1)}, u32[]{:S(2)}) copy-start(bf16[4,2,16,1024]{3,2,1,0:T(8,128)(2,1)S(1)} %pad_maximum_fusion.2.a_even) | copy-start | bytes 786436
  30.3 5.6 %collective-permute-start.3 = (bf16[4,2,16,1024]{3,2,1,0:T(8,128)(2,1)S(1)}, bf16[4,2,16,1024]{3,2,1,0:T(8,128)(2,1)S(1)}, u32[]{:S(2)}, u32[]{:S(2)}) collective-permute-start(bf16[4,2,16,1024]{3,2,1,0:T(8,128)(2,1)S(1)} %pad_maximum_fusion.2.a_even), channel_id=1, source_target_pairs={{0,1},{1,0},{2,3},{3,2},{4,5},{5,4},{6,7},{7,6},{8,9},{9,8},{10,11... | collective-permute-start | bytes 786440 | tf_op jit(solution)/shard_map/ppermute | solution.py:20
  35.9 0.7 %copy-start.5 = (bf16[4,2,16,1024]{3,2,1,0:T(8,128)(2,1)}, bf16[4,2,16,1024]{3,2,1,0:T(8,128)(2,1)S(1)}, u32[]{:S(2)}) copy-start(bf16[4,2,16,1024]{3,2,1,0:T(8,128)(2,1)S(1)} %collective-permute-done.3.a_odd) | copy-start | bytes 786436
  36.6 0.9 %copy-start.2 = (bf16[2,3,2,32,1024]{4,3,2,1,0:T(8,128)(2,1)}, bf16[2,3,2,32,1024]{4,3,2,1,0:T(8,128)(2,1)S(1)}, u32[]{:S(2)}) copy-start(bf16[2,3,2,32,1024]{4,3,2,1,0:T(8,128)(2,1)S(1)} %collective-permute-done.7.b_odd) | copy-start | bytes 2359300
  41.5 6.9 %copy-start.7 = (f32[16]{0:T(128)S(1)}, f32[16]{0:T(128)}, u32[]{:S(2)}) copy-start(f32[16]{0:T(128)} %param.11) | copy-start | bytes 196
  41.5 10.6 %collective-permute-start.8 = (bf16[6,2,128,128]{3,2,1,0:T(8,128)(2,1)}, bf16[6,2,128,128]{3,2,1,0:T(8,128)(2,1)S(1)}, u32[]{:S(2)}, u32[]{:S(2)}) collective-permute-start(bf16[6,2,128,128]{3,2,1,0:T(8,128)(2,1)} %correlate.1.own), channel_id=1, source_target_pairs={{0,8},{8,0},{16,24},{24,16},{1,9},{9,1},{17,25},{25,17},{2,10},{10... | collective-permute-start | bytes 1179656 | tf_op jit(solution)/shard_map/ppermute | solution.py:20
  44.6 9.3 %collective-permute-start.9 = (bf16[6,2,128,128]{3,2,1,0:T(8,128)(2,1)}, bf16[6,2,128,128]{3,2,1,0:T(8,128)(2,1)S(1)}, u32[]{:S(2)}, u32[]{:S(2)}) collective-permute-start(bf16[6,2,128,128]{3,2,1,0:T(8,128)(2,1)} %correlate.1.own), channel_id=1, source_target_pairs={{8,16},{16,8},{9,17},{17,9},{10,18},{18,10},{11,19},{19,11},{12,20... | collective-permute-start | bytes 1179656 | tf_op jit(solution)/shard_map/ppermute | solution.py:26
  52.1 1.8 %copy-start.3 = (bf16[6,2,128,128]{3,2,1,0:T(8,128)(2,1)}, bf16[6,2,128,128]{3,2,1,0:T(8,128)(2,1)S(1)}, u32[]{:S(2)}) copy-start(bf16[6,2,128,128]{3,2,1,0:T(8,128)(2,1)S(1)} %collective-permute-done.8.near) | copy-start | bytes 1179652
  53.9 0.8 %copy-start.4 = (bf16[6,2,128,128]{3,2,1,0:T(8,128)(2,1)}, bf16[6,2,128,128]{3,2,1,0:T(8,128)(2,1)S(1)}, u32[]{:S(2)}) copy-start(bf16[6,2,128,128]{3,2,1,0:T(8,128)(2,1)S(1)} %collective-permute-done.9.far) | copy-start | bytes 1179652
where the time goes:
time: 66.4 us; the launch traced here: 66.1 us
  waiting for transfers between devices  23.4 us (35%)
  starting transfers between devices  19.5 us (29%)
  Pallas kernels  18.4 us (28%)
  local copies, waits for them, and re-layouts  3.03 us (5%)
  other arithmetic  1.07 us (2%)
  between operations  0.73 us (1%)
    ppermute x8, waiting for transfers between devices, swap(): return lax.ppermute(block, axis, [(i, i ^ mask) for i in range(count)])  21.6 us
    ppermute x8, starting transfers between devices, swap(): return lax.ppermute(block, axis, [(i, i ^ mask) for i in range(count)])  15.7 us
    pallas_call x1, Pallas kernels, convolve(): pl.pallas_call(functools.partial(conv_kernel, n_a, n_b), out_shape=jax.Sh...  11.4 us
    pallas_call x1, Pallas kernels, correlate(): pl.pallas_call(corr_kernel, out_shape=jax.ShapeDtypeStruct((rows_b + 4, r...  3.96 us
    ppermute x2, starting transfers between devices, neighbours(): far = lax.ppermute(block, axis, across + [(j, i) for i, j in across])  3.78 us
    pallas_call x1, Pallas kernels, bands(): pl.pallas_call(body, out_shape=(jax.ShapeDtypeStruct((hid * STEP, 27 * WI...  3.03 us
    unnamed x16, local copies, waits for them, and re-layouts  2.36 us
    ppermute x2, waiting for transfers between devices, neighbours(): far = lax.ppermute(block, axis, across + [(j, i) for i, j in across])  1.8 us
  transfers between devices with their start and end apart: 10, of which 6 were waited for; matrix products, arithmetic and copies ran while one was open for 1% of the time, Pallas kernels for 5%

commit v1 on v0

v1 whole, which is shorter than its diff:
```python
import functools

import jax
import jax.numpy as jnp
import numpy as np
from jax import lax
from jax.experimental import pallas as pl
from jax.experimental.pallas import tpu as pltpu
from jax.sharding import PartitionSpec as P


WIN = 16
STEP = WIN - 2
VMEM = pltpu.VMEM
SMEM = pltpu.SMEM


def resident(*arrays):
    return [pltpu.with_memory_space_constraint(x, VMEM) for x in arrays]


def swap(block, axis, mask):
    count = lax.axis_size(axis)
    return lax.ppermute(block, axis, [(i, i ^ mask) for i in range(count)])


def neighbours(block, axis):
    count = lax.axis_size(axis)
    across = [(i, i + 1) for i in range(1, count - 1, 2)]
    far = lax.ppermute(block, axis, across + [(j, i) for i, j in across])
    return swap(block, axis, 1), far


def gathered(block, axis):
    count = lax.axis_size(axis)
    even = jnp.stack([block] + [swap(block, axis, mask) for mask in range(2, count, 2)])
    return even, swap(even, axis, 1)


def normalize(values):
    values = values.astype(jnp.float32)
    scale = lax.rsqrt(jnp.sum(values * values, axis=-1, keepdims=True) + 1e-06)
    return (values * scale).astype(jnp.bfloat16)


def corr_kernel(a_even, a_odd, b_even, b_odd, out, all_a, all_b):
    at_a, at_b = lax.axis_index("ra"), lax.axis_index("rb")
    odd = at_b & 1
    rows_b = b_even.shape[2]
    ext = all_b.shape[0]
    begins = (2, (1 - odd) * (ext - 2), odd * (ext - 2))
    skips = (0, odd * (rows_b - 2), (1 - odd) * (rows_b - 2))
    for low, (a_in, b_in) in enumerate(((a_even, b_even), (a_odd, b_odd))):
        cols = a_in.shape[2]
        for m in range(a_in.shape[0]):
            source = at_b ^ (2 * m + low)
            start = pl.multiple_of(source * cols, cols)
            all_a[:, pl.ds(start, cols), :] = normalize(a_in[m]).astype(all_a.dtype)
        cols = b_in.shape[3]
        for m in range(b_in.shape[0]):
            source = at_a ^ (2 * m + low)
            start = pl.multiple_of(source * cols, cols)
            for side in range(3):
                for k in range(2 if side else rows_b):
                    row = b_in[m, side, skips[side] + k]
                    all_b[begins[side] + k, pl.ds(start, cols), :] = normalize(row).astype(all_b.dtype)
    rows_a, wide_a, channels = all_a.shape
    wide_b = all_b.shape[1]
    flat_a = all_a[...].astype(jnp.bfloat16).reshape(rows_a * wide_a, channels)
    for k in range(0, ext, 2):
        product = lax.dot_general(
            flat_a,
            all_b[k : k + 2].astype(jnp.bfloat16).reshape(2 * wide_b, channels),
            (((1,), (1,)), ((), ())),
            preferred_element_type=jnp.float32,
        ).astype(jnp.bfloat16)
        for h in range(2):
            for i in range(rows_a):
                out[k + h, i] = product[i * wide_a : (i + 1) * wide_a, h * wide_b : (h + 1) * wide_b]


def correlate(a_even, a_odd, b_even, b_odd):
    half_a, rows_a, cols_a, channels = a_even.shape
    half_b, _, rows_b, cols_b, _ = b_even.shape
    wide_a, wide_b = 2 * half_a * cols_a, 2 * half_b * cols_b
    kind_a = jnp.bfloat16 if cols_a % 16 == 0 else jnp.float32
    kind_b = jnp.bfloat16 if cols_b % 16 == 0 else jnp.float32
    return pl.pallas_call(
        corr_kernel,
        out_shape=VMEM((rows_b + 4, rows_a, wide_a, wide_b), jnp.bfloat16),
        in_specs=[pl.BlockSpec(memory_space=VMEM)] * 4,
        out_specs=pl.BlockSpec(memory_space=VMEM),
        scratch_shapes=[
            VMEM((rows_a, wide_a, channels), kind_a),
            VMEM((rows_b + 4, wide_b, channels), kind_b),
        ],
        name="correlate",
    )(*resident(a_even, a_odd, b_even, b_odd))


def band_tables(hid):
    taps = np.arange(81)[:, None]
    col = np.arange(27 * WIN)[None]
    pick = np.zeros((2, 3, 81, 27 * WIN), np.float32)
    for p in range(2):
        along = col // (9 * WIN) if p else 2 - col // (9 * WIN)
        same = (taps // 27 == along) & (taps // 3 % 3 == col // (3 * WIN) % 3) & (taps % 3 == col // WIN % 3)
        for b in range(3):
            pick[p, b] = same & (taps // 9 % 3 == b)
    grow = np.arange(hid * STEP)[:, None] // STEP == np.arange(hid)[None]
    return pick, grow.astype(np.float32)


def band_kernel(tail, pick, grow, w1, w2, bias, band1, band2, bias_full):
    odd = lax.axis_index("ra") & 1
    rows, cols = band1.shape
    hid = w1.shape[0]

    def masked(parts, jj, ww):
        reach = ww - jj
        total = jnp.where(reach == 0, parts[0], 0.0)
        for b in (1, 2):
            total = total + jnp.where(reach == b, parts[b], 0.0)
        return total

    column = lax.broadcasted_iota(jnp.int32, (rows, 1), 0)
    group = sum((column >= STEP * o).astype(jnp.int32) for o in range(1, hid))
    parts = [
        jnp.dot(
            grow[...],
            jnp.dot(w1[...], pick[odd, b], preferred_element_type=jnp.float32).astype(jnp.bfloat16),
            preferred_element_type=jnp.float32,
        )
        for b in range(3)
    ]
    across = lax.broadcasted_iota(jnp.int32, (1, cols), 1) & (WIN - 1)
    band1[...] = masked(parts, column - STEP * group, across).astype(jnp.bfloat16)
    total = jnp.zeros(bias_full.shape, jnp.float32)
    for o in range(hid):
        total = jnp.where(group == o, bias[o], total)
    bias_full[...] = total

    row = lax.broadcasted_iota(jnp.int32, (1, rows), 1)
    jj = row - STEP * sum((row >= STEP * o).astype(jnp.int32) for o in range(1, hid))
    rr = lax.broadcasted_iota(jnp.int32, (cols, 1), 0) & (WIN - 1)
    parts = [
        lax.dot_general(
            lax.dot_general(
                pick[odd, b], w2[...], (((0,), (1,)), ((), ())), preferred_element_type=jnp.float32
            ).astype(jnp.bfloat16),
            grow[...],
            (((1,), (1,)), ((), ())),
            preferred_element_type=jnp.float32,
        )
        for b in range(3)
    ]
    total = masked(parts, rr - 2, jj)
    band2[0] = total.astype(jnp.bfloat16)
    band2[1] = jnp.where(jj < tail, total, 0.0).astype(jnp.bfloat16)


def bands(weight_one, bias_one, weight_two, width):
    hid = weight_one.shape[0]
    pick, grow = band_tables(hid)
    blocks = pl.cdiv(width, STEP)
    return pl.pallas_call(
        functools.partial(band_kernel, width - STEP * (blocks - 1)),
        out_shape=(
            VMEM((hid * STEP, 27 * WIN), jnp.bfloat16),
            VMEM((2, 27 * WIN, hid * STEP), jnp.bfloat16),
            VMEM((hid * STEP, 128), jnp.float32),
        ),
        in_specs=[pl.BlockSpec(memory_space=VMEM)] * 4 + [pl.BlockSpec(memory_space=SMEM)],
        out_specs=(pl.BlockSpec(memory_space=VMEM),) * 3,
        name="bands",
    )(jnp.asarray(pick, jnp.bfloat16), jnp.asarray(grow, jnp.bfloat16), weight_one, weight_two, bias_one)


def shifted(values, by):
    lane = lax.broadcasted_iota(jnp.int32, values.shape, values.ndim - 1)
    width = values.shape[-1]
    if by == 1:
        return jnp.where(lane == 0, 0.0, pltpu.roll(values, 1, values.ndim - 1))
    return jnp.where(lane == width - 1, 0.0, pltpu.roll(values, width - 1, values.ndim - 1))


def conv_kernel(part, unroll, n_a, n_b, *refs):
    refs = list(refs)
    own, side, band1, band2, bias1 = refs[:5]
    before, bias2 = refs[5:7] if part else (None, None)
    out, stage = refs[5 + 2 * part : 7 + 2 * part]
    total = refs[7 + 2 * part] if part else out
    windows = refs[7 + 3 * part :]
    ext_k, rows_a, width, lanes = own.shape
    rows_b = ext_k - 4
    hid_i, hid_k = rows_a + 2, rows_b + 2
    pairs = hid_k // 2
    blocks = pl.cdiv(width, STEP)
    at_a, at_b = lax.axis_index("ra"), lax.axis_index("rb")
    odd = at_a & 1

    def inside(at, count, rows, row):
        where = at * rows + row - 1
        return ((where >= 0) & (where < count * rows)).astype(jnp.float32)

    def actual(row, rows):
        return odd * row + (1 - odd) * (rows - 1 - row)

    valid_i = [inside(at_a, n_a, rows_a, actual(i, hid_i)) for i in range(hid_i)]
    valid_k = [inside(at_b, n_b, rows_b, k) for k in range(hid_k)]
    total[...] = before[...] if part else jnp.zeros_like(total)
    tall = stage.shape[2]

    def fill(k, carry):
        for i in range(4):
            stage[i, k, 0:8, :] = jnp.zeros((8, lanes), jnp.float32)
            stage[i, k, 8 + width :, :] = jnp.zeros((tall - 8 - width, lanes), jnp.float32)
        for ref, first in ((own, 0 if part else 2), (side, 2 if part else 0)):
            for i in range(2):
                stage[first + i, k, 8 : 8 + width, :] = ref[k, actual(i, rows_a)].astype(jnp.float32)
        return carry

    lax.fori_loop(0, ext_k, fill, 0)

    def build(block, window, rows):
        for i in rows:
            for k in range(ext_k):
                piece = stage[i, k, pl.ds(STEP * block + 7, WIN), :]
                for d, moved in enumerate((shifted(piece, 1), piece, shifted(piece, -1))):
                    window[i, k, d] = moved.astype(jnp.bfloat16)

    def first(i, window):
        columns = jnp.concatenate(
            [
                jnp.concatenate([window[i + a, k : k + 3].reshape(9 * WIN, lanes) for a in range(3)], axis=0)
                for k in range(hid_k)
            ],
            axis=1,
        )
        hidden = jnp.dot(band1[...], columns, preferred_element_type=jnp.float32)
        bias = bias1[...]
        return jnp.maximum(hidden + jnp.concatenate([bias] * hid_k, axis=1), 0.0).astype(jnp.bfloat16)

    def second(local, hidden, last, sums):
        i = 2 * part + local
        taps_a = [a for a in range(3) if 0 <= i - a < rows_a]
        for p in range(pairs):
            k = 2 * p
            taps_c = [c for c in range(3) if any(0 <= k + h - c < rows_b for h in range(2))]
            size = 3 * WIN
            weights = jnp.concatenate(
                [band2[last, pl.ds((3 * a + c) * size, size), :] for a in taps_a for c in taps_c], axis=0
            )
            result = jnp.dot(weights, hidden[:, k * lanes : (k + 2) * lanes], preferred_element_type=jnp.float32)
            at = 0
            for a in taps_a:
                for c in taps_c:
                    for d in range(3):
                        for h in range(2):
                            o_i, o_k = i - a, k + h - c
                            if 0 <= o_k < rows_b:
                                piece = result[at : at + WIN, h * lanes : (h + 1) * lanes]
                                if i in (0, hid_i - 1) or k + h in (0, hid_k - 1):
                                    piece = piece * (valid_i[i] * valid_k[k + h])
                                key = (o_i, o_k, d)
                                sums[key] = sums[key] + piece if key in sums else piece
                        at += WIN

    def gather(block, sums):
        for o_i in range(rows_a):
            for o_k in range(rows_b):
                rows = pl.ds(STEP * block + 7, WIN)
                total[o_i, o_k, rows, :] = total[o_i, o_k, rows, :] + (
                    shifted(sums[o_i, o_k, 0], 1) + sums[o_i, o_k, 1] + shifted(sums[o_i, o_k, 2], -1)
                )

    build(0, windows[0], range(4))

    def several(step, carry):
        pending = None
        for n in range(unroll):
            block = unroll * step + n
            last = (block == blocks - 1).astype(jnp.int32)
            sums = {}
            following = windows[(n + 1) % unroll]
            for local in range(2):
                hidden = first(local, windows[n])
                if pending is not None:
                    pending()
                build(block + 1, following, range(2 * local, 2 * local + 2))

                def pending(local=local, hidden=hidden, last=last, sums=sums, block=block):
                    second(local, hidden, last, sums)
                    if local == 1:
                        gather(block, sums)

        pending()
        return carry

    lax.fori_loop(0, blocks // unroll, several, 0)
    if part:
        for o_i in range(rows_a):
            for o_k in range(rows_b):
                out[actual(o_i, rows_a), :, o_k, :] = jnp.maximum(
                    total[o_i, o_k, 8 : 8 + width, :] + bias2[0], 0.0
                )


def convolve(part, n_a, n_b, own, side, tables, before=None, bias_two=None):
    ext_k, rows_a, width, lanes = own.shape
    rows_b = ext_k - 4
    blocks = pl.cdiv(width, STEP)
    unroll = 10
    assert rows_a == 2 and rows_b % 2 == 0 and blocks % unroll == 0
    tall = pl.cdiv(STEP * blocks + 7 + WIN, 8) * 8
    sums = (rows_a, rows_b, tall, lanes)
    here = pl.BlockSpec(memory_space=VMEM)
    return pl.pallas_call(
        functools.partial(conv_kernel, part, unroll, n_a, n_b),
        out_shape=jax.ShapeDtypeStruct((rows_a, width, rows_b, lanes), jnp.float32) if part else VMEM(sums, jnp.float32),
        in_specs=[here] * 5 + ([here, pl.BlockSpec(memory_space=SMEM)] if part else []),
        out_specs=here,
        scratch_shapes=[
            VMEM((4, ext_k, tall, lanes), jnp.float32),
        ]
        + [VMEM(sums, jnp.float32)] * part
        + [VMEM((4, ext_k, 3, WIN, lanes), jnp.bfloat16)] * unroll,
    )(*resident(own, side, *tables), *((*resident(before), bias_two) if part else ()))


def per_device(features_a, features_b, weight_one, bias_one, weight_two, bias_two):
    near_b, far_b = neighbours(features_b, "rb")
    a_even, a_odd = gathered(features_a, "rb")
    b_even, b_odd = gathered(jnp.stack([features_b, near_b, far_b]), "ra")
    tables = bands(weight_one, bias_one, weight_two, 2 * a_even.shape[0] * a_even.shape[2])
    own = correlate(a_even, a_odd, b_even, b_odd)
    near, far = neighbours(own, "ra")
    sizes = lax.axis_size("ra"), lax.axis_size("rb")
    half = convolve(0, *sizes, own, near, tables)
    return convolve(1, *sizes, own, far, tables, half, bias_two)


def solution(mesh):
    return jax.shard_map(
        per_device,
        mesh=mesh,
        in_specs=(P("ra", "rb", None), P("rb", "ra", None), P(), P(), P(), P()),
        out_specs=P("ra", None, "rb", None),
        check_vma=False,
    )
```

time: 66.4 us -> 55.3 us (0.83)
  Pallas kernels: 18.4 us -> 12.2 us
  local copies, waits for them, and re-layouts: 3.03 us -> 0.01 us
  waiting for transfers between devices: 23.4 us -> 21.6 us
    pallas_call x3 -> x4, Pallas kernels: 18.4 us -> 12.2 us  [the longest x2 8.65 us: convolve(): pl.pallas_call(functools.partial(conv_kernel, part, unroll, n_a, n_b), ou...]
    unnamed x16 -> x2, local copies, waits for them, and re-layouts: 2.36 us -> 0.01 us
    ppermute x2, waiting for transfers between devices: 1.8 us -> 0.01 us  [neighbours(): far = lax.ppermute(block, axis, across + [(j, i) for i, j in across])]
    broadcast_in_dim x1 -> x0, local copies, waits for them, and re-layouts: 0.67 us -> none  [bands(): jnp.broadcast_to(bias_one[:, None], (hid, 128))]
  transfers between devices with their start and end apart: 10 -> 10, of which waited for: 6 -> 5; matrix products, arithmetic and copies ran while one was open for 1% -> 0% of each run, Pallas kernels for 5% -> 11%
where the time goes in v1:
time: 55.3 us; the launch traced here: 55 us
  waiting for transfers between devices  21.6 us (39%)
  starting transfers between devices  19.4 us (35%)
  Pallas kernels  12.2 us (22%)
  other arithmetic  1.07 us (2%)
  between operations  0.73 us (1%)
    ppermute x8, waiting for transfers between devices, swap(): return lax.ppermute(block, axis, [(i, i ^ mask) for i in range(count)])  21.6 us
    ppermute x8, starting transfers between devices, swap(): return lax.ppermute(block, axis, [(i, i ^ mask) for i in range(count)])  15.7 us
    pallas_call x2, Pallas kernels, convolve(): pl.pallas_call(functools.partial(conv_kernel, part, unroll, n_a, n_b), ou...  8.65 us
    ppermute x2, starting transfers between devices, neighbours(): far = lax.ppermute(block, axis, across + [(j, i) for i, j in across])  3.67 us
    pallas_call x1, Pallas kernels, bands(): pl.pallas_call(functools.partial(band_kernel, width - STEP * (blocks - 1)...  2.29 us
    pallas_call x1, Pallas kernels, correlate(): pl.pallas_call(corr_kernel, out_shape=VMEM((rows_b + 4, rows_a, wide_a, w...  1.29 us
  transfers between devices with their start and end apart: 10, of which 5 were waited for; matrix products, arithmetic and copies ran while one was open for 0% of the time, Pallas kernels for 11%

profile of v1, /device:TPU:1, one launch (start us, length us, event | category | flops | bytes accessed | tf_op | source)
XLA Modules:
  0.0 55.0 jit_solution(16349588995457633165)
XLA Ops:
  0.0 2.1 %collective-permute-start.4 = (bf16[2,32,1024]{2,1,0:T(8,128)(2,1)}, bf16[2,32,1024]{2,1,0:T(8,128)(2,1)S(1)}, u32[]{:S(2)}, u32[]{:S(2)}) collective-permute-start(bf16[2,32,1024]{2,1,0:T(8,128)(2,1)} %param.9), channel_id=1, source_target_pairs={{0,1},{1,0},{2,3},{3,2},{4,5},{5,4},{6,7},{7,6},{8,9},{9,8},{10,11... | collective-permute-start | bytes 393224 | tf_op jit(solution)/shard_map/ppermute | solution.py:24
  2.1 0.7 %collective-permute-start.5 = (bf16[2,32,1024]{2,1,0:T(8,128)(2,1)}, bf16[2,32,1024]{2,1,0:T(8,128)(2,1)S(1)}, u32[]{:S(2)}, u32[]{:S(2)}) collective-permute-start(bf16[2,32,1024]{2,1,0:T(8,128)(2,1)} %param.9), channel_id=1, source_target_pairs={{1,2},{3,4},{5,6},{2,1},{4,3},{6,5},{9,10},{11,12},{13,14},{10,9},... | collective-permute-start | bytes 393224 | tf_op jit(solution)/shard_map/ppermute | solution.py:30
  2.7 2.7 %collective-permute-done.4 = bf16[2,32,1024]{2,1,0:T(8,128)(2,1)S(1)} collective-permute-done((bf16[2,32,1024]{2,1,0:T(8,128)(2,1)}, bf16[2,32,1024]{2,1,0:T(8,128)(2,1)S(1)}, u32[]{:S(2)}, u32[]{:S(2)}) %collective-permute-start.4) | collective-permute-done | bytes 131104 | tf_op jit(solution)/shard_map/ppermute | solution.py:24
  5.5 0.0 collective-permute-done.5
  5.5 1.0 %fusion = (bf16[1,3,2,32,1024]{4,3,2,1,0:T(8,128)(2,1)S(1)}, bf16[3,2,32,1024]{3,2,1,0:T(8,128)(2,1)S(1)}) fusion(bf16[1,2,32,1024]{3,2,1,0:T(8,128)(2,1)S(1)} %bitcast.13, bf16[1,2,32,1024]{3,2,1,0:T(8,128)(2,1)S(1)} %bitcast.12, bf16[1,2,32,1024]{3,2,1,0:T(8,128)(2,1)} %bitcast.11), kind=kLoop, calls=%fused_computation.3 | loop fusion | flops 393216 | bytes 1179648 | tf_op jit(solution)/shard_map/stack | solution.py:36
  6.4 1.2 %collective-permute-start.6 = (bf16[3,2,32,1024]{3,2,1,0:T(8,128)(2,1)S(1)}, bf16[3,2,32,1024]{3,2,1,0:T(8,128)(2,1)S(1)}, u32[]{:S(2)}, u32[]{:S(2)}) collective-permute-start(bf16[3,2,32,1024]{3,2,1,0:T(8,128)(2,1)S(1)} %get-tuple-element.12), channel_id=1, source_target_pairs={{0,16},{8,24},{16,0},{24,8},{1,17},{9,25},{17,1},{25,9},{2,18},{10... | collective-permute-start | bytes 1179656 | tf_op jit(solution)/shard_map/ppermute | solution.py:24
  7.7 8.3 %collective-permute-done.6 = bf16[3,2,32,1024]{3,2,1,0:T(8,128)(2,1)S(1)} collective-permute-done((bf16[3,2,32,1024]{3,2,1,0:T(8,128)(2,1)S(1)}, bf16[3,2,32,1024]{3,2,1,0:T(8,128)(2,1)S(1)}, u32[]{:S(2)}, u32[]{:S(2)}) %collective-permute-start.6) | collective-permute-done | bytes 393248 | tf_op jit(solution)/shard_map/ppermute | solution.py:24
  15.9 0.1 pad_maximum_fusion.b_even
  16.0 2.2 %collective-permute-start.7 = (bf16[2,3,2,32,1024]{4,3,2,1,0:T(8,128)(2,1)S(1)}, bf16[2,3,2,32,1024]{4,3,2,1,0:T(8,128)(2,1)S(1)}, u32[]{:S(2)}, u32[]{:S(2)}) collective-permute-start(bf16[2,3,2,32,1024]{4,3,2,1,0:T(8,128)(2,1)S(1)} %pad_maximum_fusion.b_even), channel_id=1, source_target_pairs={{0,8},{8,0},{16,24},{24,16},{1,9},{9,1},{17,25},{25,17},{2,10},{10... | collective-permute-start | bytes 2359304 | tf_op jit(solution)/shard_map/ppermute | solution.py:24
  18.2 4.7 %collective-permute-start = (bf16[2,16,1024]{2,1,0:T(8,128)(2,1)S(1)}, bf16[2,16,1024]{2,1,0:T(8,128)(2,1)S(1)}, u32[]{:S(2)}, u32[]{:S(2)}) collective-permute-start(bf16[2,16,1024]{2,1,0:T(8,128)(2,1)S(1)} %copy-done), channel_id=1, source_target_pairs={{0,2},{1,3},{2,0},{3,1},{4,6},{5,7},{6,4},{7,5},{8,10},{9,11},{10,... | collective-permute-start | bytes 196616 | tf_op jit(solution)/shard_map/ppermute | solution.py:24
  22.9 2.3 %collective-permute-start.1 = (bf16[2,16,1024]{2,1,0:T(8,128)(2,1)S(1)}, bf16[2,16,1024]{2,1,0:T(8,128)(2,1)S(1)}, u32[]{:S(2)}, u32[]{:S(2)}) collective-permute-start(bf16[2,16,1024]{2,1,0:T(8,128)(2,1)S(1)} %copy-done), channel_id=1, source_target_pairs={{0,4},{1,5},{2,6},{3,7},{4,0},{5,1},{6,2},{7,3},{8,12},{9,13},{10,... | collective-permute-start | bytes 196616 | tf_op jit(solution)/shard_map/ppermute | solution.py:24
  25.2 0.0 collective-permute-start.2
  25.2 2.3 %collective-permute-done.1 = bf16[2,16,1024]{2,1,0:T(8,128)(2,1)S(1)} collective-permute-done((bf16[2,16,1024]{2,1,0:T(8,128)(2,1)S(1)}, bf16[2,16,1024]{2,1,0:T(8,128)(2,1)S(1)}, u32[]{:S(2)}, u32[]{:S(2)}) %collective-permute-start.1) | collective-permute-done | bytes 65568 | tf_op jit(solution)/shard_map/ppermute | solution.py:24
  27.5 2.7 %collective-permute-done.2 = bf16[2,16,1024]{2,1,0:T(8,128)(2,1)S(1)} collective-permute-done((bf16[2,16,1024]{2,1,0:T(8,128)(2,1)S(1)}, bf16[2,16,1024]{2,1,0:T(8,128)(2,1)S(1)}, u32[]{:S(2)}, u32[]{:S(2)}) %collective-permute-start.2) | collective-permute-done | bytes 65568 | tf_op jit(solution)/shard_map/ppermute | solution.py:24
  30.2 0.1 collective-permute-start.3
  30.3 5.5 %collective-permute-done.3.a_odd = bf16[4,2,16,1024]{3,2,1,0:T(8,128)(2,1)S(1)} collective-permute-done((bf16[4,2,16,1024]{3,2,1,0:T(8,128)(2,1)S(1)}, bf16[4,2,16,1024]{3,2,1,0:T(8,128)(2,1)S(1)}, u32[]{:S(2)}, u32[]{:S(2)}) %collective-permute-start.3) | collective-permute-done | bytes 262176 | tf_op jit(solution)/shard_map/ppermute | solution.py:24
  35.9 0.0 collective-permute-done.7.b_odd
  35.9 1.3 %correlate.1.refs_0_ = bf16[6,2,128,128]{3,2,1,0:T(8,128)(2,1)S(1)} custom-call(bf16[4,2,16,1024]{3,2,1,0:T(8,128)(2,1)S(1)} %pad_maximum_fusion.2.a_even, bf16[4,2,16,1024]{3,2,1,0:T(8,128)(2,1)S(1)} %collective-permute-done.3.a_odd, bf16[2,3,2,32,1024]{4,3,2,1,0:T(8,128)(2,1)S(1)} %pad_maximum_fusion.b_even, ...), custom_call_target="tpu_custom_call" | custom-call | tf_op jit(solution)/shard_map/correlate/pallas_call | solution.py:88
  37.2 3.2 %collective-permute-start.9 = (bf16[6,2,128,128]{3,2,1,0:T(8,128)(2,1)S(1)}, bf16[6,2,128,128]{3,2,1,0:T(8,128)(2,1)S(1)}, u32[]{:S(2)}, u32[]{:S(2)}) collective-permute-start(bf16[6,2,128,128]{3,2,1,0:T(8,128)(2,1)S(1)} %correlate.1.refs_0_), channel_id=1, source_target_pairs={{0,8},{8,0},{16,24},{24,16},{1,9},{9,1},{17,25},{25,17},{2,10},{10... | collective-permute-start | bytes 1179656 | tf_op jit(solution)/shard_map/ppermute | solution.py:24
  40.4 3.0 %collective-permute-start.8 = (bf16[6,2,128,128]{3,2,1,0:T(8,128)(2,1)S(1)}, bf16[6,2,128,128]{3,2,1,0:T(8,128)(2,1)S(1)}, u32[]{:S(2)}, u32[]{:S(2)}) collective-permute-start(bf16[6,2,128,128]{3,2,1,0:T(8,128)(2,1)S(1)} %correlate.1.refs_0_), channel_id=1, source_target_pairs={{8,16},{16,8},{9,17},{17,9},{10,18},{18,10},{11,19},{19,11},{12,20... | collective-permute-start | bytes 1179656 | tf_op jit(solution)/shard_map/ppermute | solution.py:30
  44.1 2.3 %bands.1 = (bf16[224,432]{1,0:T(8,128)(2,1)S(1)}, bf16[2,432,224]{2,1,0:T(8,128)(2,1)S(1)}, f32[224,128]{1,0:T(8,128)S(1)}) custom-call(bf16[2,3,81,432]{3,2,1,0:T(8,128)(2,1)} %constant.4.clone.pick, bf16[224,16]{1,0:T(8,128)(2,1)} %constant.5.clone.grow, bf16[16,81]{1,0:T(8,128)(2,1)} %w1.1, bf16[16,81]{1,0:T(8,128)(2,1)} %w2.1, f32[16]{0:T(128)} %bias.1), custom_call_target="tpu_custom_call" | custom-call | tf_op jit(solution)/shard_map/bands/pallas_call | solution.py:166
  46.4 0.0 collective-permute-done.9.refs_1_
  46.4 4.0 %shard_map.82.refs_5_ = f32[2,2,168,128]{3,2,1,0:T(8,128)S(1)} custom-call(bf16[6,2,128,128]{3,2,1,0:T(8,128)(2,1)S(1)} %correlate.1.refs_0_, bf16[6,2,128,128]{3,2,1,0:T(8,128)(2,1)S(1)} %collective-permute-done.9.refs_1_, bf16[224,432]{1,0:T(8,128)(2,1)S(1)} %get-tuple-element.8.refs_2_, bf16[2,432,224]{2,1,0:T(8,128)(2,1)S(1)} %get-tuple-element.9.refs_3_, ...), custom_call_target="tpu_custom_call" | custom-call | tf_op jit(solution)/shard_map/pallas_call | solution.py:318
  50.3 4.7 %shard_map.83 = f32[2,128,2,128]{3,2,1,0:T(2,128)} custom-call(bf16[6,2,128,128]{3,2,1,0:T(8,128)(2,1)S(1)} %correlate.1.refs_0_, bf16[6,2,128,128]{3,2,1,0:T(8,128)(2,1)S(1)} %collective-permute-done.8.refs_1_, bf16[224,432]{1,0:T(8,128)(2,1)S(1)} %get-tuple-element.8.refs_2_, bf16[2,432,224]{2,1,0:T(8,128)(2,1)S(1)} %get-tuple-element.9.refs_3_, ...), custom_call_target="tpu_custom_call" | custom-call | tf_op jit(solution)/shard_map/pallas_call | solution.py:318
  (5 shorter events, 0.0 us)
Async XLA Ops:
  0.0 5.5 %collective-permute-start.4 = (bf16[2,32,1024]{2,1,0:T(8,128)(2,1)}, bf16[2,32,1024]{2,1,0:T(8,128)(2,1)S(1)}, u32[]{:S(2)}, u32[]{:S(2)}) collective-permute-start(bf16[2,32,1024]{2,1,0:T(8,128)(2,1)} %param.9), channel_id=1, source_target_pairs={{0,1},{1,0},{2,3},{3,2},{4,5},{5,4},{6,7},{7,6},{8,9},{9,8},{10,11... | collective-permute-start | bytes 393224 | tf_op jit(solution)/shard_map/ppermute | solution.py:24
  2.1 3.4 %collective-permute-start.5 = (bf16[2,32,1024]{2,1,0:T(8,128)(2,1)}, bf16[2,32,1024]{2,1,0:T(8,128)(2,1)S(1)}, u32[]{:S(2)}, u32[]{:S(2)}) collective-permute-start(bf16[2,32,1024]{2,1,0:T(8,128)(2,1)} %param.9), channel_id=1, source_target_pairs={{1,2},{3,4},{5,6},{2,1},{4,3},{6,5},{9,10},{11,12},{13,14},{10,9},... | collective-permute-start | bytes 393224 | tf_op jit(solution)/shard_map/ppermute | solution.py:30
  6.4 9.5 %collective-permute-start.6 = (bf16[3,2,32,1024]{3,2,1,0:T(8,128)(2,1)S(1)}, bf16[3,2,32,1024]{3,2,1,0:T(8,128)(2,1)S(1)}, u32[]{:S(2)}, u32[]{:S(2)}) collective-permute-start(bf16[3,2,32,1024]{3,2,1,0:T(8,128)(2,1)S(1)} %get-tuple-element.12), channel_id=1, source_target_pairs={{0,16},{8,24},{16,0},{24,8},{1,17},{9,25},{17,1},{25,9},{2,18},{10... | collective-permute-start | bytes 1179656 | tf_op jit(solution)/shard_map/ppermute | solution.py:24
  15.9 2.3 %copy-start = (bf16[2,16,1024]{2,1,0:T(8,128)(2,1)S(1)}, bf16[2,16,1024]{2,1,0:T(8,128)(2,1)}, u32[]{:S(2)}) copy-start(bf16[2,16,1024]{2,1,0:T(8,128)(2,1)} %param.8) | copy-start | bytes 196612
  16.0 19.9 %collective-permute-start.7 = (bf16[2,3,2,32,1024]{4,3,2,1,0:T(8,128)(2,1)S(1)}, bf16[2,3,2,32,1024]{4,3,2,1,0:T(8,128)(2,1)S(1)}, u32[]{:S(2)}, u32[]{:S(2)}) collective-permute-start(bf16[2,3,2,32,1024]{4,3,2,1,0:T(8,128)(2,1)S(1)} %pad_maximum_fusion.b_even), channel_id=1, source_target_pairs={{0,8},{8,0},{16,24},{24,16},{1,9},{9,1},{17,25},{25,17},{2,10},{10... | collective-permute-start | bytes 2359304 | tf_op jit(solution)/shard_map/ppermute | solution.py:24
  18.2 7.0 %collective-permute-start = (bf16[2,16,1024]{2,1,0:T(8,128)(2,1)S(1)}, bf16[2,16,1024]{2,1,0:T(8,128)(2,1)S(1)}, u32[]{:S(2)}, u32[]{:S(2)}) collective-permute-start(bf16[2,16,1024]{2,1,0:T(8,128)(2,1)S(1)} %copy-done), channel_id=1, source_target_pairs={{0,2},{1,3},{2,0},{3,1},{4,6},{5,7},{6,4},{7,5},{8,10},{9,11},{10,... | collective-permute-start | bytes 196616 | tf_op jit(solution)/shard_map/ppermute | solution.py:24
  22.9 4.6 %collective-permute-start.1 = (bf16[2,16,1024]{2,1,0:T(8,128)(2,1)S(1)}, bf16[2,16,1024]{2,1,0:T(8,128)(2,1)S(1)}, u32[]{:S(2)}, u32[]{:S(2)}) collective-permute-start(bf16[2,16,1024]{2,1,0:T(8,128)(2,1)S(1)} %copy-done), channel_id=1, source_target_pairs={{0,4},{1,5},{2,6},{3,7},{4,0},{5,1},{6,2},{7,3},{8,12},{9,13},{10,... | collective-permute-start | bytes 196616 | tf_op jit(solution)/shard_map/ppermute | solution.py:24
  25.2 5.0 %collective-permute-start.2 = (bf16[2,16,1024]{2,1,0:T(8,128)(2,1)S(1)}, bf16[2,16,1024]{2,1,0:T(8,128)(2,1)S(1)}, u32[]{:S(2)}, u32[]{:S(2)}) collective-permute-start(bf16[2,16,1024]{2,1,0:T(8,128)(2,1)S(1)} %copy-done), channel_id=1, source_target_pairs={{0,6},{1,7},{2,4},{3,5},{4,2},{5,3},{6,0},{7,1},{8,14},{9,15},{10,... | collective-permute-start | bytes 196616 | tf_op jit(solution)/shard_map/ppermute | solution.py:24
  30.2 5.6 %collective-permute-start.3 = (bf16[4,2,16,1024]{3,2,1,0:T(8,128)(2,1)S(1)}, bf16[4,2,16,1024]{3,2,1,0:T(8,128)(2,1)S(1)}, u32[]{:S(2)}, u32[]{:S(2)}) collective-permute-start(bf16[4,2,16,1024]{3,2,1,0:T(8,128)(2,1)S(1)} %pad_maximum_fusion.2.a_even), channel_id=1, source_target_pairs={{0,1},{1,0},{2,3},{3,2},{4,5},{5,4},{6,7},{7,6},{8,9},{9,8},{10,11... | collective-permute-start | bytes 786440 | tf_op jit(solution)/shard_map/ppermute | solution.py:24
  37.2 9.2 %collective-permute-start.9 = (bf16[6,2,128,128]{3,2,1,0:T(8,128)(2,1)S(1)}, bf16[6,2,128,128]{3,2,1,0:T(8,128)(2,1)S(1)}, u32[]{:S(2)}, u32[]{:S(2)}) collective-permute-start(bf16[6,2,128,128]{3,2,1,0:T(8,128)(2,1)S(1)} %correlate.1.refs_0_), channel_id=1, source_target_pairs={{0,8},{8,0},{16,24},{24,16},{1,9},{9,1},{17,25},{25,17},{2,10},{10... | collective-permute-start | bytes 1179656 | tf_op jit(solution)/shard_map/ppermute | solution.py:24
  40.4 9.9 %collective-permute-start.8 = (bf16[6,2,128,128]{3,2,1,0:T(8,128)(2,1)S(1)}, bf16[6,2,128,128]{3,2,1,0:T(8,128)(2,1)S(1)}, u32[]{:S(2)}, u32[]{:S(2)}) collective-permute-start(bf16[6,2,128,128]{3,2,1,0:T(8,128)(2,1)S(1)} %correlate.1.refs_0_), channel_id=1, source_target_pairs={{8,16},{16,8},{9,17},{17,9},{10,18},{18,10},{11,19},{19,11},{12,20... | collective-permute-start | bytes 1179656 | tf_op jit(solution)/shard_map/ppermute | solution.py:30

commit v2 on v1

--- a/solution.py
+++ b/solution.py
@@ -15,6 +15,9 @@
 SMEM = pltpu.SMEM
 
 
+GRANT = 24 << 20
+
+
 def resident(*arrays):
     return [pltpu.with_memory_space_constraint(x, VMEM) for x in arrays]
 
@@ -31,10 +34,19 @@
     return swap(block, axis, 1), far
 
 
+def pieces(block, axis):
+    count = lax.axis_size(axis)
+    even = [block] + [swap(block, axis, mask) for mask in range(2, count, 2)]
+    odd = [swap(block, axis, 1)]
+    odd += [swap(x, axis, 1) for x in even[1:]]
+    return [x for pair in zip(even, odd) for x in pair]
+
+
 def gathered(block, axis):
     count = lax.axis_size(axis)
-    even = jnp.stack([block] + [swap(block, axis, mask) for mask in range(2, count, 2)])
-    return even, swap(even, axis, 1)
+    even = jnp.stack([swap(block, axis, mask) for mask in range(2, count, 2)])
+    partner = swap(block, axis, 1)
+    return block[None], partner[None], even, swap(even, axis, 1)
 
 
 def normalize(values):
@@ -43,27 +55,29 @@
     return (values * scale).astype(jnp.bfloat16)
 
 
-def corr_kernel(a_even, a_odd, b_even, b_odd, out, all_a, all_b):
+def corr_kernel(a_own, a_partner, a_even, a_odd, *refs):
     at_a, at_b = lax.axis_index("ra"), lax.axis_index("rb")
     odd = at_b & 1
-    rows_b = b_even.shape[2]
+    out, all_a, all_b = refs[-3:]
+    count = (len(refs) - 3) // 2
+    own_b, halo_b = refs[:count], refs[count:-3]
+    rows_b = own_b[0].shape[0]
     ext = all_b.shape[0]
     begins = (2, (1 - odd) * (ext - 2), odd * (ext - 2))
     skips = (0, odd * (rows_b - 2), (1 - odd) * (rows_b - 2))
-    for low, (a_in, b_in) in enumerate(((a_even, b_even), (a_odd, b_odd))):
-        cols = a_in.shape[2]
-        for m in range(a_in.shape[0]):
-            source = at_b ^ (2 * m + low)
-            start = pl.multiple_of(source * cols, cols)
-            all_a[:, pl.ds(start, cols), :] = normalize(a_in[m]).astype(all_a.dtype)
-        cols = b_in.shape[3]
-        for m in range(b_in.shape[0]):
-            source = at_a ^ (2 * m + low)
-            start = pl.multiple_of(source * cols, cols)
-            for side in range(3):
-                for k in range(2 if side else rows_b):
-                    row = b_in[m, side, skips[side] + k]
-                    all_b[begins[side] + k, pl.ds(start, cols), :] = normalize(row).astype(all_b.dtype)
+    for first, blocks in enumerate((a_own, a_partner, a_even, a_odd)):
+        cols = blocks.shape[2]
+        for m in range(blocks.shape[0]):
+            start = pl.multiple_of((at_b ^ (2 * m + first)) * cols, cols)
+            all_a[:, pl.ds(start, cols), :] = normalize(blocks[m]).astype(all_a.dtype)
+    for m in range(count):
+        cols = own_b[m].shape[1]
+        start = pl.multiple_of((at_a ^ m) * cols, cols)
+        for side in range(3):
+            for k in range(2 if side else rows_b):
+                at = skips[side] + k
+                row = halo_b[m][side - 1, at] if side else own_b[m][at]
+                all_b[begins[side] + k, pl.ds(start, cols), :] = normalize(row).astype(all_b.dtype)
     rows_a, wide_a, channels = all_a.shape
     wide_b = all_b.shape[1]
     flat_a = all_a[...].astype(jnp.bfloat16).reshape(rows_a * wide_a, channels)
@@ -79,23 +93,24 @@
                 out[k + h, i] = product[i * wide_a : (i + 1) * wide_a, h * wide_b : (h + 1) * wide_b]
 
 
-def correlate(a_even, a_odd, b_even, b_odd):
-    half_a, rows_a, cols_a, channels = a_even.shape
-    half_b, _, rows_b, cols_b, _ = b_even.shape
-    wide_a, wide_b = 2 * half_a * cols_a, 2 * half_b * cols_b
+def correlate(parts_a, own_b, halo_b):
+    _, rows_a, cols_a, channels = parts_a[0].shape
+    rows_b, cols_b, _ = own_b[0].shape
+    wide_a, wide_b = sum(x.shape[0] for x in parts_a) * cols_a, len(own_b) * cols_b
     kind_a = jnp.bfloat16 if cols_a % 16 == 0 else jnp.float32
     kind_b = jnp.bfloat16 if cols_b % 16 == 0 else jnp.float32
     return pl.pallas_call(
         corr_kernel,
         out_shape=VMEM((rows_b + 4, rows_a, wide_a, wide_b), jnp.bfloat16),
-        in_specs=[pl.BlockSpec(memory_space=VMEM)] * 4,
+        in_specs=[pl.BlockSpec(memory_space=VMEM)] * (4 + 2 * len(own_b)),
         out_specs=pl.BlockSpec(memory_space=VMEM),
         scratch_shapes=[
             VMEM((rows_a, wide_a, channels), kind_a),
             VMEM((rows_b + 4, wide_b, channels), kind_b),
         ],
+        compiler_params=pltpu.CompilerParams(vmem_limit_bytes=GRANT),
         name="correlate",
-    )(*resident(a_even, a_odd, b_even, b_odd))
+    )(*resident(*parts_a, *own_b, *halo_b))
 
 
 def band_tables(hid):
@@ -172,6 +187,7 @@
         ),
         in_specs=[pl.BlockSpec(memory_space=VMEM)] * 4 + [pl.BlockSpec(memory_space=SMEM)],
         out_specs=(pl.BlockSpec(memory_space=VMEM),) * 3,
+        compiler_params=pltpu.CompilerParams(vmem_limit_bytes=GRANT),
         name="bands",
     )(jnp.asarray(pick, jnp.bfloat16), jnp.asarray(grow, jnp.bfloat16), weight_one, weight_two, bias_one)
 
@@ -325,15 +341,18 @@
         ]
         + [VMEM(sums, jnp.float32)] * part
         + [VMEM((4, ext_k, 3, WIN, lanes), jnp.bfloat16)] * unroll,
+        compiler_params=pltpu.CompilerParams(vmem_limit_bytes=GRANT),
     )(*resident(own, side, *tables), *((*resident(before), bias_two) if part else ()))
 
 
 def per_device(features_a, features_b, weight_one, bias_one, weight_two, bias_two):
-    near_b, far_b = neighbours(features_b, "rb")
-    a_even, a_odd = gathered(features_a, "rb")
-    b_even, b_odd = gathered(jnp.stack([features_b, near_b, far_b]), "ra")
-    tables = bands(weight_one, bias_one, weight_two, 2 * a_even.shape[0] * a_even.shape[2])
-    own = correlate(a_even, a_odd, b_even, b_odd)
+    parts_a = gathered(features_a, "rb")
+    sides = neighbours(features_b, "rb")
+    own_b = pieces(features_b, "ra")
+    sides = jnp.stack(sides)
+    halo_b = pieces(sides, "ra")
+    tables = bands(weight_one, bias_one, weight_two, lax.axis_size("rb") * features_a.shape[1])
+    own = correlate(parts_a, own_b, halo_b)
     near, far = neighbours(own, "ra")
     sizes = lax.axis_size("ra"), lax.axis_size("rb")
     half = convolve(0, *sizes, own, near, tables)

time: 55.3 us -> 43.9 us (0.79)
  waiting for transfers between devices: 21.6 us -> 6.94 us
  starting transfers between devices: 19.4 us -> 24.3 us
  other arithmetic: 1.07 us -> 0.05 us
    ppermute x8 -> x13, waiting for transfers between devices: 21.6 us -> 6.54 us  [swap(): return lax.ppermute(block, axis, [(i, i ^ mask) for i in range(count)])]
    ppermute x8 -> x13, starting transfers between devices: 15.7 us -> 21.3 us  [swap(): return lax.ppermute(block, axis, [(i, i ^ mask) for i in range(count)])]
    another operation x3 -> x2, other arithmetic: 1.07 us -> 0.05 us  [the longest x1 0.03 us: per_device(): sides = jnp.stack(sides)]
    ppermute x2, starting transfers between devices: 3.67 us -> 2.92 us  [neighbours(): far = lax.ppermute(block, axis, across + [(j, i) for i, j in across])]
    pallas_call x1, Pallas kernels: 2.29 us -> 1.73 us  [bands(): pl.pallas_call(functools.partial(band_kernel, width - STEP * (blocks - 1)...]
  transfers between devices with their start and end apart: 10 -> 15, of which waited for: 5 -> 5; matrix products, arithmetic and copies ran while one was open for 0% -> 0% of each run, Pallas kernels for 11% -> 13%
where the time goes in v2:
time: 43.9 us; the launch traced here: 43.8 us
  starting transfers between devices  24.3 us (55%)
  Pallas kernels  11.7 us (27%)
  waiting for transfers between devices  6.94 us (16%)
  between operations  0.82 us (2%)
    ppermute x13, starting transfers between devices, swap(): return lax.ppermute(block, axis, [(i, i ^ mask) for i in range(count)])  21.3 us
    pallas_call x2, Pallas kernels, convolve(): pl.pallas_call(functools.partial(conv_kernel, part, unroll, n_a, n_b), ou...  8.65 us
    ppermute x13, waiting for transfers between devices, swap(): return lax.ppermute(block, axis, [(i, i ^ mask) for i in range(count)])  6.54 us
    ppermute x2, starting transfers between devices, neighbours(): far = lax.ppermute(block, axis, across + [(j, i) for i, j in across])  2.92 us
    pallas_call x1, Pallas kernels, bands(): pl.pallas_call(functools.partial(band_kernel, width - STEP * (blocks - 1)...  1.73 us
    pallas_call x1, Pallas kernels, correlate(): pl.pallas_call(corr_kernel, out_shape=VMEM((rows_b + 4, rows_a, wide_a, w...  1.29 us
  transfers between devices with their start and end apart: 15, of which 5 were waited for; matrix products, arithmetic and copies ran while one was open for 0% of the time, Pallas kernels for 13%

profile of v2, /device:TPU:1, one launch (start us, length us, event | category | flops | bytes accessed | tf_op | source)
XLA Modules:
  0.0 43.8 jit_solution(11947929569357132258)
XLA Ops:
  0.0 2.1 %collective-permute-start.8 = (bf16[2,32,1024]{2,1,0:T(8,128)(2,1)}, bf16[2,32,1024]{2,1,0:T(8,128)(2,1)S(1)}, u32[]{:S(2)}, u32[]{:S(2)}) collective-permute-start(bf16[2,32,1024]{2,1,0:T(8,128)(2,1)} %refs_0_.1), channel_id=1, source_target_pairs={{0,1},{1,0},{2,3},{3,2},{4,5},{5,4},{6,7},{7,6},{8,9},{9,8},{10,11... | collective-permute-start | bytes 393224 | tf_op jit(solution)/shard_map/ppermute | solution.py:27
  2.1 0.7 %collective-permute-start.9 = (bf16[2,32,1024]{2,1,0:T(8,128)(2,1)}, bf16[2,32,1024]{2,1,0:T(8,128)(2,1)S(1)}, u32[]{:S(2)}, u32[]{:S(2)}) collective-permute-start(bf16[2,32,1024]{2,1,0:T(8,128)(2,1)} %refs_0_.1), channel_id=1, source_target_pairs={{1,2},{3,4},{5,6},{2,1},{4,3},{6,5},{9,10},{11,12},{13,14},{10,9},... | collective-permute-start | bytes 393224 | tf_op jit(solution)/shard_map/ppermute | solution.py:33
  2.7 2.7 %collective-permute-done.8 = bf16[2,32,1024]{2,1,0:T(8,128)(2,1)S(1)} collective-permute-done((bf16[2,32,1024]{2,1,0:T(8,128)(2,1)}, bf16[2,32,1024]{2,1,0:T(8,128)(2,1)S(1)}, u32[]{:S(2)}, u32[]{:S(2)}) %collective-permute-start.8) | collective-permute-done | bytes 131104 | tf_op jit(solution)/shard_map/ppermute | solution.py:27
  5.5 1.2 %collective-permute-start.11 = (bf16[2,2,32,1024]{3,2,1,0:T(8,128)(2,1)S(1)}, bf16[2,2,32,1024]{3,2,1,0:T(8,128)(2,1)S(1)}, u32[]{:S(2)}, u32[]{:S(2)}) collective-permute-start(bf16[2,2,32,1024]{3,2,1,0:T(8,128)(2,1)S(1)} %pad_maximum_fusion.refs_4_), channel_id=1, source_target_pairs={{0,16},{8,24},{16,0},{24,8},{1,17},{9,25},{17,1},{25,9},{2,18},{10... | collective-permute-start | bytes 786440 | tf_op jit(solution)/shard_map/ppermute | solution.py:27
  6.7 4.7 %collective-permute-start.1 = (bf16[2,16,1024]{2,1,0:T(8,128)(2,1)S(1)}, bf16[2,16,1024]{2,1,0:T(8,128)(2,1)S(1)}, u32[]{:S(2)}, u32[]{:S(2)}) collective-permute-start(bf16[2,16,1024]{2,1,0:T(8,128)(2,1)S(1)} %copy-done.2), channel_id=1, source_target_pairs={{0,2},{1,3},{2,0},{3,1},{4,6},{5,7},{6,4},{7,5},{8,10},{9,11},{10,... | collective-permute-start | bytes 196616 | tf_op jit(solution)/shard_map/ppermute | solution.py:27
  11.5 2.3 %collective-permute-start.2 = (bf16[2,16,1024]{2,1,0:T(8,128)(2,1)S(1)}, bf16[2,16,1024]{2,1,0:T(8,128)(2,1)S(1)}, u32[]{:S(2)}, u32[]{:S(2)}) collective-permute-start(bf16[2,16,1024]{2,1,0:T(8,128)(2,1)S(1)} %copy-done.2), channel_id=1, source_target_pairs={{0,4},{1,5},{2,6},{3,7},{4,0},{5,1},{6,2},{7,3},{8,12},{9,13},{10,... | collective-permute-start | bytes 196616 | tf_op jit(solution)/shard_map/ppermute | solution.py:27
  13.8 0.7 %collective-permute-start.6 = (bf16[2,32,1024]{2,1,0:T(8,128)(2,1)S(1)}, bf16[2,32,1024]{2,1,0:T(8,128)(2,1)S(1)}, u32[]{:S(2)}, u32[]{:S(2)}) collective-permute-start(bf16[2,32,1024]{2,1,0:T(8,128)(2,1)S(1)} %copy-done.1), channel_id=1, source_target_pairs={{0,16},{8,24},{16,0},{24,8},{1,17},{9,25},{17,1},{25,9},{2,18},{10... | collective-permute-start | bytes 393224 | tf_op jit(solution)/shard_map/ppermute | solution.py:27
  14.5 0.2 collective-permute-start
  14.7 1.5 %collective-permute-done.2 = bf16[2,16,1024]{2,1,0:T(8,128)(2,1)S(1)} collective-permute-done((bf16[2,16,1024]{2,1,0:T(8,128)(2,1)S(1)}, bf16[2,16,1024]{2,1,0:T(8,128)(2,1)S(1)}, u32[]{:S(2)}, u32[]{:S(2)}) %collective-permute-start.2) | collective-permute-done | bytes 65568 | tf_op jit(solution)/shard_map/ppermute | solution.py:27
  16.2 4.5 %collective-permute-start.10 = (bf16[2,2,32,1024]{3,2,1,0:T(8,128)(2,1)S(1)}, bf16[2,2,32,1024]{3,2,1,0:T(8,128)(2,1)S(1)}, u32[]{:S(2)}, u32[]{:S(2)}) collective-permute-start(bf16[2,2,32,1024]{3,2,1,0:T(8,128)(2,1)S(1)} %pad_maximum_fusion.refs_4_), channel_id=1, source_target_pairs={{0,8},{8,0},{16,24},{24,16},{1,9},{9,1},{17,25},{25,17},{2,10},{10... | collective-permute-start | bytes 786440 | tf_op jit(solution)/shard_map/ppermute | solution.py:27
  20.8 0.1 collective-permute-start.4
  20.8 2.1 %collective-permute-start.5 = (bf16[2,32,1024]{2,1,0:T(8,128)(2,1)S(1)}, bf16[2,32,1024]{2,1,0:T(8,128)(2,1)S(1)}, u32[]{:S(2)}, u32[]{:S(2)}) collective-permute-start(bf16[2,32,1024]{2,1,0:T(8,128)(2,1)S(1)} %copy-done.1), channel_id=1, source_target_pairs={{0,8},{8,0},{16,24},{24,16},{1,9},{9,1},{17,25},{25,17},{2,10},{10... | collective-permute-start | bytes 393224 | tf_op jit(solution)/shard_map/ppermute | solution.py:27
  23.0 0.1 collective-permute-start.7
  23.1 0.9 %collective-permute-done.5.refs_1_ = bf16[2,32,1024]{2,1,0:T(8,128)(2,1)S(1)} collective-permute-done((bf16[2,32,1024]{2,1,0:T(8,128)(2,1)S(1)}, bf16[2,32,1024]{2,1,0:T(8,128)(2,1)S(1)}, u32[]{:S(2)}, u32[]{:S(2)}) %collective-permute-start.5) | collective-permute-done | bytes 131104 | tf_op jit(solution)/shard_map/ppermute | solution.py:27
  24.0 1.4 %collective-permute-done.4.a_odd = bf16[3,2,16,1024]{3,2,1,0:T(8,128)(2,1)S(1)} collective-permute-done((bf16[3,2,16,1024]{3,2,1,0:T(8,128)(2,1)S(1)}, bf16[3,2,16,1024]{3,2,1,0:T(8,128)(2,1)S(1)}, u32[]{:S(2)}, u32[]{:S(2)}) %collective-permute-start.4) | collective-permute-done | bytes 196640 | tf_op jit(solution)/shard_map/ppermute | solution.py:27
  25.4 0.0 copy-start
  25.4 0.0 copy-start.3
  25.4 1.3 %correlate.1.refs_0_ = bf16[6,2,128,128]{3,2,1,0:T(8,128)(2,1)S(1)} custom-call(bf16[1,2,16,1024]{3,2,1,0:T(8,128)(2,1)S(1)} %bitcast.7, bf16[1,2,16,1024]{3,2,1,0:T(8,128)(2,1)S(1)} %bitcast.8, bf16[3,2,16,1024]{3,2,1,0:T(8,128)(2,1)S(1)} %pad_maximum_fusion.1.a_even, bf16[3,2,16,1024]{3,2,1,0:T(8,128)(2,1)S(1)} %collective-permute-done.4.a_odd, ...), custom_call_target="tpu_custom_call" | custom-call | tf_op jit(solution)/shard_map/correlate/pallas_call | solution.py:102
  26.7 3.3 %collective-permute-start.14 = (bf16[6,2,128,128]{3,2,1,0:T(8,128)(2,1)S(1)}, bf16[6,2,128,128]{3,2,1,0:T(8,128)(2,1)S(1)}, u32[]{:S(2)}, u32[]{:S(2)}) collective-permute-start(bf16[6,2,128,128]{3,2,1,0:T(8,128)(2,1)S(1)} %correlate.1.refs_0_), channel_id=1, source_target_pairs={{0,8},{8,0},{16,24},{24,16},{1,9},{9,1},{17,25},{25,17},{2,10},{10... | collective-permute-start | bytes 1179656 | tf_op jit(solution)/shard_map/ppermute | solution.py:27
  30.0 2.3 %collective-permute-start.13 = (bf16[6,2,128,128]{3,2,1,0:T(8,128)(2,1)S(1)}, bf16[6,2,128,128]{3,2,1,0:T(8,128)(2,1)S(1)}, u32[]{:S(2)}, u32[]{:S(2)}) collective-permute-start(bf16[6,2,128,128]{3,2,1,0:T(8,128)(2,1)S(1)} %correlate.1.refs_0_), channel_id=1, source_target_pairs={{8,16},{16,8},{9,17},{17,9},{10,18},{18,10},{11,19},{19,11},{12,20... | collective-permute-start | bytes 1179656 | tf_op jit(solution)/shard_map/ppermute | solution.py:33
  33.0 1.7 %bands.1 = (bf16[224,432]{1,0:T(8,128)(2,1)S(1)}, bf16[2,432,224]{2,1,0:T(8,128)(2,1)S(1)}, f32[224,128]{1,0:T(8,128)S(1)}) custom-call(bf16[2,3,81,432]{3,2,1,0:T(8,128)(2,1)S(1)} %copy-done, bf16[224,16]{1,0:T(8,128)(2,1)S(1)} %copy-done.3, bf16[16,81]{1,0:T(8,128)(2,1)S(1)} %copy-done.4, bf16[16,81]{1,0:T(8,128)(2,1)S(1)} %copy-done.5, f32[16]{0:T(128)S(1)} %copy-done.6), custom_call_target="tpu_custom_call" | custom-call | tf_op jit(solution)/shard_map/bands/pallas_call | solution.py:181
  34.7 4.0 %shard_map.82.refs_5_ = f32[2,2,168,128]{3,2,1,0:T(8,128)S(1)} custom-call(bf16[6,2,128,128]{3,2,1,0:T(8,128)(2,1)S(1)} %correlate.1.refs_0_, bf16[6,2,128,128]{3,2,1,0:T(8,128)(2,1)S(1)} %collective-permute-done.14.refs_1_, bf16[224,432]{1,0:T(8,128)(2,1)S(1)} %get-tuple-element.8.refs_2_, bf16[2,432,224]{2,1,0:T(8,128)(2,1)S(1)} %get-tuple-element.9.refs_3_, ...), custom_call_target="tpu_custom_call" | custom-call | tf_op jit(solution)/shard_map/pallas_call | solution.py:334
  38.7 0.4 collective-permute-done.13.refs_1_
  39.1 4.7 %shard_map.83 = f32[2,128,2,128]{3,2,1,0:T(2,128)} custom-call(bf16[6,2,128,128]{3,2,1,0:T(8,128)(2,1)S(1)} %correlate.1.refs_0_, bf16[6,2,128,128]{3,2,1,0:T(8,128)(2,1)S(1)} %collective-permute-done.13.refs_1_, bf16[224,432]{1,0:T(8,128)(2,1)S(1)} %get-tuple-element.8.refs_2_, bf16[2,432,224]{2,1,0:T(8,128)(2,1)S(1)} %get-tuple-element.9.refs_3_, ...), custom_call_target="tpu_custom_call" | custom-call | tf_op jit(solution)/shard_map/pallas_call | solution.py:334
  (26 shorter events, 0.1 us)
Async XLA Ops:
  0.0 5.5 %collective-permute-start.8 = (bf16[2,32,1024]{2,1,0:T(8,128)(2,1)}, bf16[2,32,1024]{2,1,0:T(8,128)(2,1)S(1)}, u32[]{:S(2)}, u32[]{:S(2)}) collective-permute-start(bf16[2,32,1024]{2,1,0:T(8,128)(2,1)} %refs_0_.1), channel_id=1, source_target_pairs={{0,1},{1,0},{2,3},{3,2},{4,5},{5,4},{6,7},{7,6},{8,9},{9,8},{10,11... | collective-permute-start | bytes 393224 | tf_op jit(solution)/shard_map/ppermute | solution.py:27
  2.1 3.4 %collective-permute-start.9 = (bf16[2,32,1024]{2,1,0:T(8,128)(2,1)}, bf16[2,32,1024]{2,1,0:T(8,128)(2,1)S(1)}, u32[]{:S(2)}, u32[]{:S(2)}) collective-permute-start(bf16[2,32,1024]{2,1,0:T(8,128)(2,1)} %refs_0_.1), channel_id=1, source_target_pairs={{1,2},{3,4},{5,6},{2,1},{4,3},{6,5},{9,10},{11,12},{13,14},{10,9},... | collective-permute-start | bytes 393224 | tf_op jit(solution)/shard_map/ppermute | solution.py:33
  5.5 1.3 %copy-start.2 = (bf16[2,16,1024]{2,1,0:T(8,128)(2,1)S(1)}, bf16[2,16,1024]{2,1,0:T(8,128)(2,1)}, u32[]{:S(2)}) copy-start(bf16[2,16,1024]{2,1,0:T(8,128)(2,1)} %param.8) | copy-start | bytes 196612
  5.5 8.3 %copy-start.1 = (bf16[2,32,1024]{2,1,0:T(8,128)(2,1)S(1)}, bf16[2,32,1024]{2,1,0:T(8,128)(2,1)}, u32[]{:S(2)}) copy-start(bf16[2,32,1024]{2,1,0:T(8,128)(2,1)} %refs_0_.1) | copy-start | bytes 393220
  5.5 15.2 %collective-permute-start.11 = (bf16[2,2,32,1024]{3,2,1,0:T(8,128)(2,1)S(1)}, bf16[2,2,32,1024]{3,2,1,0:T(8,128)(2,1)S(1)}, u32[]{:S(2)}, u32[]{:S(2)}) collective-permute-start(bf16[2,2,32,1024]{3,2,1,0:T(8,128)(2,1)S(1)} %pad_maximum_fusion.refs_4_), channel_id=1, source_target_pairs={{0,16},{8,24},{16,0},{24,8},{1,17},{9,25},{17,1},{25,9},{2,18},{10... | collective-permute-start | bytes 786440 | tf_op jit(solution)/shard_map/ppermute | solution.py:27
  6.7 7.8 %collective-permute-start.1 = (bf16[2,16,1024]{2,1,0:T(8,128)(2,1)S(1)}, bf16[2,16,1024]{2,1,0:T(8,128)(2,1)S(1)}, u32[]{:S(2)}, u32[]{:S(2)}) collective-permute-start(bf16[2,16,1024]{2,1,0:T(8,128)(2,1)S(1)} %copy-done.2), channel_id=1, source_target_pairs={{0,2},{1,3},{2,0},{3,1},{4,6},{5,7},{6,4},{7,5},{8,10},{9,11},{10,... | collective-permute-start | bytes 196616 | tf_op jit(solution)/shard_map/ppermute | solution.py:27
  11.5 4.7 %collective-permute-start.2 = (bf16[2,16,1024]{2,1,0:T(8,128)(2,1)S(1)}, bf16[2,16,1024]{2,1,0:T(8,128)(2,1)S(1)}, u32[]{:S(2)}, u32[]{:S(2)}) collective-permute-start(bf16[2,16,1024]{2,1,0:T(8,128)(2,1)S(1)} %copy-done.2), channel_id=1, source_target_pairs={{0,4},{1,5},{2,6},{3,7},{4,0},{5,1},{6,2},{7,3},{8,12},{9,13},{10,... | collective-permute-start | bytes 196616 | tf_op jit(solution)/shard_map/ppermute | solution.py:27
  13.8 6.9 %collective-permute-start.3 = (bf16[2,16,1024]{2,1,0:T(8,128)(2,1)S(1)}, bf16[2,16,1024]{2,1,0:T(8,128)(2,1)S(1)}, u32[]{:S(2)}, u32[]{:S(2)}) collective-permute-start(bf16[2,16,1024]{2,1,0:T(8,128)(2,1)S(1)} %copy-done.2), channel_id=1, source_target_pairs={{0,6},{1,7},{2,4},{3,5},{4,2},{5,3},{6,0},{7,1},{8,14},{9,15},{10,... | collective-permute-start | bytes 196616 | tf_op jit(solution)/shard_map/ppermute | solution.py:27
  13.8 9.2 %collective-permute-start.6 = (bf16[2,32,1024]{2,1,0:T(8,128)(2,1)S(1)}, bf16[2,32,1024]{2,1,0:T(8,128)(2,1)S(1)}, u32[]{:S(2)}, u32[]{:S(2)}) collective-permute-start(bf16[2,32,1024]{2,1,0:T(8,128)(2,1)S(1)} %copy-done.1), channel_id=1, source_target_pairs={{0,16},{8,24},{16,0},{24,8},{1,17},{9,25},{17,1},{25,9},{2,18},{10... | collective-permute-start | bytes 393224 | tf_op jit(solution)/shard_map/ppermute | solution.py:27
  14.5 6.3 %collective-permute-start = (bf16[2,16,1024]{2,1,0:T(8,128)(2,1)S(1)}, bf16[2,16,1024]{2,1,0:T(8,128)(2,1)S(1)}, u32[]{:S(2)}, u32[]{:S(2)}) collective-permute-start(bf16[2,16,1024]{2,1,0:T(8,128)(2,1)S(1)} %copy-done.2), channel_id=1, source_target_pairs={{0,1},{1,0},{2,3},{3,2},{4,5},{5,4},{6,7},{7,6},{8,9},{9,8},{10,11... | collective-permute-start | bytes 196616 | tf_op jit(solution)/shard_map/ppermute | solution.py:27
  16.2 9.2 %collective-permute-start.10 = (bf16[2,2,32,1024]{3,2,1,0:T(8,128)(2,1)S(1)}, bf16[2,2,32,1024]{3,2,1,0:T(8,128)(2,1)S(1)}, u32[]{:S(2)}, u32[]{:S(2)}) collective-permute-start(bf16[2,2,32,1024]{3,2,1,0:T(8,128)(2,1)S(1)} %pad_maximum_fusion.refs_4_), channel_id=1, source_target_pairs={{0,8},{8,0},{16,24},{24,16},{1,9},{9,1},{17,25},{25,17},{2,10},{10... | collective-permute-start | bytes 786440 | tf_op jit(solution)/shard_map/ppermute | solution.py:27
  20.7 4.6 %collective-permute-start.12 = (bf16[2,2,32,1024]{3,2,1,0:T(8,128)(2,1)S(1)}, bf16[2,2,32,1024]{3,2,1,0:T(8,128)(2,1)S(1)}, u32[]{:S(2)}, u32[]{:S(2)}) collective-permute-start(bf16[2,2,32,1024]{3,2,1,0:T(8,128)(2,1)S(1)} %collective-permute-done.11.refs_6_), channel_id=1, source_target_pairs={{0,8},{8,0},{16,24},{24,16},{1,9},{9,1},{17,25},{25,17},{2,10},{10... | collective-permute-start | bytes 786440 | tf_op jit(solution)/shard_map/ppermute | solution.py:27
  20.8 4.6 %collective-permute-start.4 = (bf16[3,2,16,1024]{3,2,1,0:T(8,128)(2,1)S(1)}, bf16[3,2,16,1024]{3,2,1,0:T(8,128)(2,1)S(1)}, u32[]{:S(2)}, u32[]{:S(2)}) collective-permute-start(bf16[3,2,16,1024]{3,2,1,0:T(8,128)(2,1)S(1)} %pad_maximum_fusion.1.a_even), channel_id=1, source_target_pairs={{0,1},{1,0},{2,3},{3,2},{4,5},{5,4},{6,7},{7,6},{8,9},{9,8},{10,11... | collective-permute-start | bytes 589832 | tf_op jit(solution)/shard_map/ppermute | solution.py:27
  20.8 3.1 %collective-permute-start.5 = (bf16[2,32,1024]{2,1,0:T(8,128)(2,1)S(1)}, bf16[2,32,1024]{2,1,0:T(8,128)(2,1)S(1)}, u32[]{:S(2)}, u32[]{:S(2)}) collective-permute-start(bf16[2,32,1024]{2,1,0:T(8,128)(2,1)S(1)} %copy-done.1), channel_id=1, source_target_pairs={{0,8},{8,0},{16,24},{24,16},{1,9},{9,1},{17,25},{25,17},{2,10},{10... | collective-permute-start | bytes 393224 | tf_op jit(solution)/shard_map/ppermute | solution.py:27
  23.0 2.4 %collective-permute-start.7 = (bf16[2,32,1024]{2,1,0:T(8,128)(2,1)S(1)}, bf16[2,32,1024]{2,1,0:T(8,128)(2,1)S(1)}, u32[]{:S(2)}, u32[]{:S(2)}) collective-permute-start(bf16[2,32,1024]{2,1,0:T(8,128)(2,1)S(1)} %collective-permute-done.6.refs_2_), channel_id=1, source_target_pairs={{0,8},{8,0},{16,24},{24,16},{1,9},{9,1},{17,25},{25,17},{2,10},{10... | collective-permute-start | bytes 393224 | tf_op jit(solution)/shard_map/ppermute | solution.py:27
  25.4 7.6 %copy-start = (bf16[2,3,81,432]{3,2,1,0:T(8,128)(2,1)S(1)}, bf16[2,3,81,432]{3,2,1,0:T(8,128)(2,1)}, u32[]{:S(2)}) copy-start(bf16[2,3,81,432]{3,2,1,0:T(8,128)(2,1)} %constant.4.clone.pick) | copy-start | bytes 1259716
  25.4 7.6 %copy-start.3 = (bf16[224,16]{1,0:T(8,128)(2,1)S(1)}, bf16[224,16]{1,0:T(8,128)(2,1)}, u32[]{:S(2)}) copy-start(bf16[224,16]{1,0:T(8,128)(2,1)} %constant.5.clone.grow) | copy-start | bytes 21508
  25.4 7.6 %copy-start.4 = (bf16[16,81]{1,0:T(8,128)(2,1)S(1)}, bf16[16,81]{1,0:T(8,128)(2,1)}, u32[]{:S(2)}) copy-start(bf16[16,81]{1,0:T(8,128)(2,1)} %w1.1) | copy-start | bytes 7780
  25.4 7.6 %copy-start.5 = (bf16[16,81]{1,0:T(8,128)(2,1)S(1)}, bf16[16,81]{1,0:T(8,128)(2,1)}, u32[]{:S(2)}) copy-start(bf16[16,81]{1,0:T(8,128)(2,1)} %w2.1) | copy-start | bytes 7780
  26.7 6.3 %copy-start.6 = (f32[16]{0:T(128)S(1)}, f32[16]{0:T(128)}, u32[]{:S(2)}) copy-start(f32[16]{0:T(128)} %bias.1) | copy-start | bytes 196
  26.7 8.0 %collective-permute-start.14 = (bf16[6,2,128,128]{3,2,1,0:T(8,128)(2,1)S(1)}, bf16[6,2,128,128]{3,2,1,0:T(8,128)(2,1)S(1)}, u32[]{:S(2)}, u32[]{:S(2)}) collective-permute-start(bf16[6,2,128,128]{3,2,1,0:T(8,128)(2,1)S(1)} %correlate.1.refs_0_), channel_id=1, source_target_pairs={{0,8},{8,0},{16,24},{24,16},{1,9},{9,1},{17,25},{25,17},{2,10},{10... | collective-permute-start | bytes 1179656 | tf_op jit(solution)/shard_map/ppermute | solution.py:27
  30.0 9.1 %collective-permute-start.13 = (bf16[6,2,128,128]{3,2,1,0:T(8,128)(2,1)S(1)}, bf16[6,2,128,128]{3,2,1,0:T(8,128)(2,1)S(1)}, u32[]{:S(2)}, u32[]{:S(2)}) collective-permute-start(bf16[6,2,128,128]{3,2,1,0:T(8,128)(2,1)S(1)} %correlate.1.refs_0_), channel_id=1, source_target_pairs={{8,16},{16,8},{9,17},{17,9},{10,18},{18,10},{11,19},{19,11},{12,20... | collective-permute-start | bytes 1179656 | tf_op jit(solution)/shard_map/ppermute | solution.py:33
